TPU v7x, 32 devices: a whole 2x2x4 slice. The times are simulated.
32 devices in a mesh: rep: 4 (over y, x), shard: 8 (over z, core).
Axes of the slice: x: 2, y: 2, z: 4, core: 2. Of those that a mesh axis runs over, the one named last changes fastest.
Arguments:
- tokens: bfloat16 [12288, 768], P(('rep', 'shard')), may hold values from -6 to 6
- routes: int32 [12288], P(('rep', 'shard')), may hold values from 0 to 7, as said below
- slot_ids: int32 [12288], P(('rep', 'shard')), may hold values from 0 to 95, as said below
- w_query: bfloat16 [768, 768], P('shard'), may hold values from -0.21875 to 0.21875
- w_key: bfloat16 [768, 768], P('shard'), may hold values from -0.21875 to 0.21875
- w_value: bfloat16 [768, 768], P('shard'), may hold values from -0.21875 to 0.21875
- w_output: bfloat16 [768, 768], P('shard'), may hold values from -3 to 3
- w_router: bfloat16 [768, 8], P('shard'), may hold values from -0.15625 to 0.15625
- norm_attn: bfloat16 [768], P('shard'), may hold values from 0.5 to 1.5
- norm_moe: bfloat16 [768], P('shard'), may hold values from 0.5 to 1.5
- rel_table: bfloat16 [32, 12], P('shard'), may hold values from -4 to 4
- w_in: bfloat16 [8, 768, 3072], P('shard'), may hold values from -0.21875 to 0.21875
- w_out: bfloat16 [8, 3072, 768], P('shard'), may hold values from -2.390625 to 2.390625
- cotangent: bfloat16 [12288, 768], P(('rep', 'shard')), may hold values from -6 to 6
Outputs:
- mixed: bfloat16 [12288, 768], P(('rep', 'shard'))
- grad_tokens: float32 [12288, 768], P(('rep', 'shard'))
- grad_w_query: float32 [768, 768], P('shard')
- grad_w_key: float32 [768, 768], P('shard')
- grad_w_value: float32 [768, 768], P('shard')
- grad_w_output: float32 [768, 768], P('shard')
- grad_w_router: float32 [768, 8], P('shard')
- grad_norm_attn: float32 [768], P('shard')
- grad_norm_moe: float32 [768], P('shard')
- grad_rel_table: float32 [32, 12], P('shard')
- grad_w_in: float32 [8, 768, 3072], P('shard', 'rep')
- grad_w_out: float32 [8, 3072, 768], P('shard', 'rep')
Inputs may be any that keep to these rules, and one draw needn't show every extreme that they name: `routes`: in each device's block of 384 tokens no expert is named more than 96 times; in every group one expert, drawn from the seed, is named exactly 96 times in each of the group's blocks. `slot_ids`: within a block, tokens with the same route have different slots.
All inputs are finite; a program needn't handle non-finite values.
Results may differ from a plain program's by a relative error of at most 0.024.
Values may be sent and summed in bfloat16 or wider, within the bound.
A program may use at most 256 MiB of HBM per device.

v0:
```python
import jax
import jax.numpy as jnp
import numpy as np
from jax import lax
from jax.experimental import pallas as pl
from jax.experimental.pallas import tpu as pltpu
from jax.sharding import PartitionSpec as P

PR_DEV = 128
TILE = 128
SPAN = 2 * TILE
BLOCK = 1536
NEAR = 3
QUARTERS = 4
far_before, far_after, causal_tile, hidden_tile, tile_kinds = 3, 4, 5, 6, 7
vmem_cap = 60 * 1024 * 1024
mesh_ids = pl.DeviceIdType.MESH
bucket_edges = (12, 16, 23, 32, 46, 64, 91)
norm_epsilon = 1e-06
masked_score = -1e30
low, single = jnp.bfloat16, jnp.float32
in_vmem = pl.BlockSpec(memory_space=pltpu.VMEM)
anywhere = pl.BlockSpec(memory_space=pl.ANY)


def inverse_rms(values):
    return lax.rsqrt(jnp.mean(values * values, axis=-1, keepdims=True) + norm_epsilon)


def norm_pull(grad, values, gain):
    scale = inverse_rms(values)
    pulled = grad * gain
    mean = jnp.mean(pulled * values, axis=-1, keepdims=True)
    return scale * pulled - values * (scale * scale * scale * mean)


def nt(left, right):
    return lax.dot_general(left, right, (((1,), (1,)), ((), ())), preferred_element_type=single)


def tn(left, right):
    return lax.dot_general(left, right, (((0,), (0,)), ((), ())), preferred_element_type=single)


def nn(left, right):
    return jnp.dot(left, right, preferred_element_type=single)


def thirds_of(values):
    first = values.astype(low)
    rest = values - first.astype(single)
    second = rest.astype(low)
    return first, second, (rest - second.astype(single)).astype(low)


def fill_tiles(tiles_ref, rev_row, low, high):
    spread = jnp.broadcast_to(rev_row, (TILE, 4 * TILE))
    rolled = pltpu.roll(spread, 0, 1, stride=1, stride_axis=0)
    keys = lax.broadcasted_iota(jnp.int32, (TILE, TILE), 0)
    rows = lax.broadcasted_iota(jnp.int32, (TILE, TILE), 1)
    tiles_ref[0] = rolled[:, TILE : 2 * TILE]
    tiles_ref[1] = rolled[:, :TILE]
    tiles_ref[2] = rolled[:, 3 * TILE :]
    tiles_ref[far_before] = jnp.broadcast_to(low, (TILE, TILE))
    tiles_ref[far_after] = jnp.broadcast_to(high, (TILE, TILE))
    tiles_ref[causal_tile] = jnp.where(keys <= rows, rolled[:, :TILE], masked_score)
    tiles_ref[hidden_tile] = jnp.full((TILE, TILE), masked_score, jnp.float32)


def prompt_tile(block, chunk, shard_id, block_count):
    if chunk == 0:
        gap = block - shard_id
        far = jnp.where(gap < 0, far_before, far_after)
        return jnp.where(jnp.abs(gap) <= 1, gap + 1, far)
    if chunk == 1 and block == block_count - 1:
        return jnp.where(shard_id % 2 == 0, 0, far_before)
    return far_before


def local_tile(block, chunk, shard_id):
    if block >= 2:
        return ((causal_tile, 0), (hidden_tile, causal_tile))[block - 2][chunk]
    kind = 0 if (block, chunk) == (1, 0) else far_before
    return jnp.where(shard_id % 2 == 1, kind, hidden_tile)


def prompt_grid(part, shard_id, block_count):
    return [
        [(side, prompt_tile(2 * part + half, chunk, shard_id, block_count)) for side in range(2) for chunk in range(3)]
        for half in range(2)
    ]


def local_grid(part, shard_id):
    return [
        [(side, local_tile(2 * part + half, chunk, shard_id)) for side in range(2) for chunk in range(2)]
        for half in range(2)
    ]


def tile_of(values, i, j):
    return values[i * TILE : (i + 1) * TILE, j * TILE : (j + 1) * TILE]


def with_bias(scores, tiles_ref, grid):
    lines = [
        jnp.concatenate(
            [tile_of(scores, i, j) + tiles_ref[side, kind] for j, (side, kind) in enumerate(row)], axis=1
        )
        for i, row in enumerate(grid)
    ]
    return jnp.concatenate(lines, axis=0)


def both_heads(values):
    first = head_mask(values.shape[0], 0)
    none = jnp.zeros_like(values)
    return jnp.concatenate([jnp.where(first, values, none), jnp.where(first, none, values)], axis=0)


def continuation(values, axis):
    rows = values.shape[axis] // 2
    pick = (lambda a, b: values[:, a:b]) if axis else (lambda a, b: values[a:b])
    return jnp.concatenate([pick(PR_DEV, rows), pick(rows + PR_DEV, 2 * rows)], axis=axis)


def fold8(values):
    return values.reshape(values.shape[0] // 8, 8, values.shape[1])


def head_mask(rows, side):
    lanes = lax.broadcasted_iota(jnp.int32, (rows, TILE), 1)
    return (lanes < TILE // 2) if side == 0 else (lanes >= TILE // 2)


def distance_buckets(bucket_count):
    steps = np.arange(4 * TILE)
    gap = -np.where(steps < 2 * TILE, steps, steps - 4 * TILE)
    size = np.abs(gap)
    far = sum((size >= edge).astype(np.int64) for edge in bucket_edges)
    exact = bucket_count // 4
    return np.where(gap > 0, bucket_count // 2, 0) + np.where(size < exact, size, exact + far)


def front_kernel(
    ints_ref, bucket_ref, cot_ref, wq_hbm, wk_hbm, wv_hbm, wo_hbm, tok_hbm, little_hbm,
    lse_ref, rev_ref, gate_ref, col_ref, gain_ref, x_ref, gin_hbm, w_hbm, every_hbm, small_hbm,
    n_hbm, q_hbm, k_hbm, v_hbm, o_hbm, mid_hbm,
    tiles, vt, sp, sl, gbuf, w_ref, every_ref, small_ref, tok_ref, shard_w, little,
    n_ref, nt_ref, q_ref, k_ref, v_ref, ot_ref, mid_ref,
    gs, gr, loc, wz_s, wz_r, tz_s, tz_r, sz_s, sz_r, wr_s, wr_r, wt_s, wt_r, tt_s, tt_r, st_s, st_r, et_s, et_r,
):
    rep, chip, core, chips, quarter = places()
    along, across, twin = peer_lists()
    shards = chips * 2
    shard_id = chip * 2 + core
    rows, width = tok_ref.shape
    experts = shards
    blocks = every_ref.shape[0] // TILE - 4
    half = TILE // 2
    heads_held = rev_ref.shape[0]
    lines = shard_w.shape[1]
    rest_rows = rows - PR_DEV
    prompt_len = blocks * TILE
    others = [(rep, (shard_id + k) % shards) for k in range(1, shards)]

    def w_rows(source, side):
        return pl.ds(pl.multiple_of((source * 2 + side) * lines, lines), lines)

    def t_rows(source, side):
        return every_ref.at[pl.ds(pl.multiple_of((source * 2 + side) * PR_DEV, PR_DEV), PR_DEV)]

    loads = [
        pltpu.make_async_copy(source, shard_w.at[i], loc.at[i])
        for i, source in enumerate((wq_hbm, wk_hbm, wv_hbm, wo_hbm))
    ] + [pltpu.make_async_copy(tok_hbm, tok_ref, loc.at[4]), pltpu.make_async_copy(little_hbm, little, loc.at[5])]
    for copy in loads:
        copy.start()
    greeted = [twin] + along
    for device in across + [(rep, (chip + k) % chips * 2 + 1 - core) for k in range(1, chips)]:
        greeted.append(device)
    greet(greeted)
    started = []

    def go(source, target, sems, device):
        copy = send(source, target, sems, device)
        copy.start()
        started.append(copy)

    def landed(piece, sems):
        send(piece, piece, sems, twin).wait_recv()

    for copy in loads:
        copy.wait()
    mine = w_rows(chip, core)
    prompt, rest = tok_ref.at[pl.ds(0, PR_DEV)], tok_ref.at[pl.ds(PR_DEV, rest_rows)]
    for k, device in enumerate(along):
        go(shard_w.at[quarter], w_ref.at[quarter, mine], (wz_s.at[k], wz_r.at[k]), device)
        go(little, small_ref.at[mine], (sz_s.at[k], sz_r.at[k]), device)
    go(little, small_ref.at[mine], (st_s.at[0], st_r.at[0]), twin)
    go(rest, every_ref.at[pl.ds(prompt_len, rest_rows)], (et_s.at[0], et_r.at[0]), twin)
    go(prompt, t_rows(chip, core), (tt_s.at[0], tt_r.at[0]), twin)
    go(shard_w, w_ref.at[:, mine], (wt_s.at[0], wt_r.at[0]), twin)
    w_ref[:, mine, :] = shard_w[...]
    small_ref[mine, :] = little[...]
    every_ref[pl.ds(pl.multiple_of(shard_id * PR_DEV, PR_DEV), PR_DEV), :] = tok_ref[:PR_DEV, :]
    every_ref[prompt_len + rest_rows :, :] = tok_ref[PR_DEV:, :]
    ints = ints_ref[...].astype(single).T
    route_col = ints[:, 0:1].astype(jnp.int32)
    col_ref[...] = jnp.broadcast_to(ints[:, 1:2].astype(jnp.int32), col_ref.shape)
    slots = lax.broadcasted_iota(jnp.int32, (x_ref.shape[0], rows), 0)
    place = (slots == ints_ref[1:2, :]).astype(low)
    gbuf[...] = nn(place, cot_ref[...]).astype(low).reshape(gbuf.shape)
    own_g = pltpu.make_async_copy(gbuf.at[shard_id], gin_hbm.at[shard_id], loc.at[6])
    own_g.start()

    for k in range(1, chips):
        source = (chip + chips - k) % chips
        piece = w_ref.at[quarter, w_rows(source, core)]
        landed(piece, (wz_s.at[k - 1], wz_r.at[k - 1]))
        for j, device in enumerate(across):
            go(piece, piece, (wr_s.at[k - 1, j], wr_r.at[k - 1, j]), device)
        go(prompt, t_rows(chip, core), (tz_s.at[k - 1], tz_r.at[k - 1]), along[k - 1])
    for k in range(1, chips):
        source = (chip + chips - k) % chips
        piece = small_ref.at[w_rows(source, core)]
        landed(piece, (sz_s.at[k - 1], sz_r.at[k - 1]))
        go(piece, piece, (st_s.at[k], st_r.at[k]), twin)
    for k in range(1, chips):
        source = (chip + chips - k) % chips
        piece = t_rows(source, core)
        landed(piece, (tz_s.at[k - 1], tz_r.at[k - 1]))
        go(piece, piece, (tt_s.at[k], tt_r.at[k]), twin)
    for k, device in enumerate(others):
        go(gbuf.at[device[1]], gin_hbm.at[shard_id], (gs.at[k], gr.at[k]), device)
    for k in range(chips):
        source = (chip + chips - k) % chips
        landed(small_ref.at[w_rows(source, 1 - core)], (st_s.at[k], st_r.at[k]))
    writes = []

    def write(source, target):
        writes.append(pltpu.make_async_copy(source, target, loc.at[7 + len(writes)]))
        writes[-1].start()

    write(small_ref, small_hbm)

    small_t = small_ref[...].astype(single).T
    gain_attn = small_t[experts : experts + 1]
    gain_moe = small_t[experts + 1 : experts + 2]
    gain_ref[...] = jnp.concatenate([gain_attn, gain_moe, jnp.zeros((6, width), single)], axis=0)
    shard_rows = width // shards
    table_rows = 2 * TILE // 8 // shards
    owner = lax.broadcasted_iota(jnp.int32, (shards, shard_rows, 4 * TILE), 0)
    offset = lax.broadcasted_iota(jnp.int32, (shards, shard_rows, 4 * TILE), 1)
    held = jnp.where(offset < table_rows, owner * table_rows + offset, -1).reshape(width, 4 * TILE)
    hot = (held == bucket_ref[0:1, :]).astype(low)
    table_t = small_t[experts + 2 : experts + 2 + heads_held].astype(low)
    rev_ref[...] = nn(table_t, hot)

    for k in range(chips):
        source = (chip + chips - k) % chips
        landed(t_rows(source, 1 - core), (tt_s.at[k], tt_r.at[k]))
    landed(every_ref.at[pl.ds(prompt_len, rest_rows)], (et_s.at[0], et_r.at[0]))
    write(every_ref, every_hbm)

    @pl.loop(0, every_ref.shape[0] // SPAN)
    def scale(part):
        span = pl.ds(pl.multiple_of(part * SPAN, SPAN), SPAN)
        values = every_ref[span, :].astype(single)
        normed = values * inverse_rms(values) * gain_attn
        n_ref[span, :] = normed.astype(low)
        nt_ref[:, span] = normed.T.astype(low)

    write(nt_ref, n_hbm)
    for k in range(1, chips):
        source = (chip + chips - k) % chips
        for j in range(1, QUARTERS):
            piece = w_ref.at[(quarter + QUARTERS - j) % QUARTERS, w_rows(source, core)]
            landed(piece, (wr_s.at[k - 1, j - 1], wr_r.at[k - 1, j - 1]))
        piece = w_ref.at[:, w_rows(source, core)]
        go(piece, piece, (wt_s.at[k], wt_r.at[k]), twin)
    for k in range(chips):
        source = (chip + chips - k) % chips
        landed(w_ref.at[:, w_rows(source, 1 - core)], (wt_s.at[k], wt_r.at[k]))
    write(w_ref, w_hbm)

    @pl.loop(0, every_ref.shape[0] // (2 * SPAN))
    def project(part):
        span = pl.ds(pl.multiple_of(part * 2 * SPAN, 2 * SPAN), 2 * SPAN)
        k_ref[span, :] = nn(n_ref[span, :], w_ref[1]).astype(low)
        v_ref[span, :] = nn(n_ref[span, :], w_ref[2]).astype(low)

    own = pl.ds(pl.multiple_of(shard_id * TILE, TILE), TILE)
    normed = jnp.concatenate([n_ref[own, :], n_ref[(blocks + 2) * TILE :, :]], axis=0)
    q_ref[...] = (nn(normed, w_ref[0]).astype(low) * jnp.asarray(0.125, low)).astype(low)
    write(k_ref, k_hbm)
    write(v_ref, v_hbm)
    write(q_ref, q_hbm)

    @pl.loop(0, width // TILE)
    def pair_loop(pair):
        cols = pl.ds(pl.multiple_of(pair * TILE, TILE), TILE)
        vt[...] = v_ref[:, cols].T
        q_both = both_heads(q_ref[:, cols])
        q_local = continuation(q_both, 0)
        for side in range(2):
            rev_row = rev_ref[pl.ds(pair * 2 + side, 1), :]
            fill_tiles(tiles.at[side], rev_row, rev_row[:, SPAN - 1 : SPAN], rev_row[:, SPAN : SPAN + 1])
        top = jnp.full((8, 2 * rows), masked_score, single)
        for part in range(blocks // 2):
            keys = slice(part * SPAN, (part + 1) * SPAN)
            scores = with_bias(nt(k_ref[keys, cols], q_both), tiles, prompt_grid(part, shard_id, blocks))
            sp[keys, :] = scores
            top = jnp.maximum(top, jnp.max(fold8(scores), axis=0))
        local = continuation(top, 1)
        for part in range(2):
            keys = slice(part * SPAN, (part + 1) * SPAN)
            held = slice((blocks // 2 + part) * SPAN, (blocks // 2 + part + 1) * SPAN)
            scores = with_bias(nt(k_ref[held, cols], q_local), tiles, local_grid(part, shard_id))
            sl[keys, :] = scores
            local = jnp.maximum(local, jnp.max(fold8(scores), axis=0))
        rest = rows - PR_DEV
        top = jnp.concatenate(
            [top[:, :PR_DEV], local[:, :rest], top[:, rows : rows + PR_DEV], local[:, rest:]], axis=1
        )
        top = jnp.max(top, axis=0, keepdims=True)
        total = jnp.zeros((8, 2 * rows), single)
        summed = [jnp.zeros((half, rows), single)] * 2
        for part in range(blocks // 2):
            keys = slice(part * SPAN, (part + 1) * SPAN)
            weights = jnp.exp(sp[keys, :] - top)
            total = total + jnp.sum(fold8(weights), axis=0)
            weights = weights.astype(low)
            for side in range(2):
                heads = slice(side * half, (side + 1) * half)
                summed[side] = summed[side] + nn(vt[heads, keys], weights[:, side * rows : (side + 1) * rows])
        top_local, total_local = continuation(top, 1), continuation(total, 1)
        summed_local = [part_sum[:, PR_DEV:] for part_sum in summed]
        for part in range(2):
            keys = slice(part * SPAN, (part + 1) * SPAN)
            held = slice((blocks // 2 + part) * SPAN, (blocks // 2 + part + 1) * SPAN)
            weights = jnp.exp(sl[keys, :] - top_local)
            total_local = total_local + jnp.sum(fold8(weights), axis=0)
            weights = weights.astype(low)
            for side in range(2):
                heads = slice(side * half, (side + 1) * half)
                summed_local[side] = summed_local[side] + nn(
                    vt[heads, held], weights[:, side * rest : (side + 1) * rest]
                )
        for side in range(2):
            head = pair * 2 + side
            ours = slice(side * rows, (side + 1) * rows)
            sums = jnp.concatenate(
                [total[:, side * rows : side * rows + PR_DEV], total_local[:, side * rest : (side + 1) * rest]], axis=1
            )
            sums = jnp.sum(sums, axis=0, keepdims=True)
            mixed = jnp.concatenate([summed[side][:, :PR_DEV], summed_local[side]], axis=1)
            ot_ref[pl.ds(pl.multiple_of(head * half, half), half), :] = mixed / sums
            lse_ref[pl.ds(head, 1), :] = top[:, ours] + jnp.log(sums)

    resid_mid = tok_ref[...].astype(single) + nn(ot_ref[...].T.astype(low), w_ref[3])
    mid_ref[...] = resid_mid
    write(ot_ref, o_hbm)
    write(mid_ref, mid_hbm)
    mid_low = (resid_mid * inverse_rms(resid_mid) * gain_moe).astype(low)
    probs = router_softmax(mid_low, small_ref[...], experts)
    lanes = lax.broadcasted_iota(jnp.int32, probs.shape, 1)
    gate = jnp.sum(jnp.where(lanes == route_col, probs, 0.0), axis=1, keepdims=True)
    gate_ref[...] = jnp.broadcast_to(gate, gate_ref.shape)
    x_ref[...] = nn(place, mid_low).astype(low)
    own_g.wait()
    for k in range(shards - 1):
        landed(gin_hbm.at[(shard_id + shards - k - 1) % shards], (gs.at[k], gr.at[k]))
    for copy in writes:
        copy.wait()
    for copy in started:
        copy.wait_send()


def router_softmax(rows_low, small, experts):
    logits = nn(rows_low, small)
    lanes = lax.broadcasted_iota(jnp.int32, logits.shape, 1)
    logits = jnp.where(lanes < experts, logits, masked_score)
    powers = jnp.exp(logits - jnp.max(logits, axis=1, keepdims=True))
    return powers / jnp.sum(powers, axis=1, keepdims=True)


def front(ints, bucket_row, cotangent, weights, tokens, small, slot_count):
    rows, width = tokens.shape
    shards = lax.axis_size("shard")
    chips, count = shards // 2, shards // 2 - 1
    keys = shards * PR_DEV + 2 * (rows - PR_DEV)
    lines = small.shape[0]
    shape = jax.ShapeDtypeStruct
    sem = pltpu.SemaphoreType.DMA
    vm = pltpu.VMEM
    return pl.pallas_call(
        front_kernel,
        out_shape=(
            shape((16, rows), single), shape((16, 4 * TILE), single), shape((rows, TILE), single),
            shape((rows, TILE), jnp.int32), shape((8, width), single), shape((slot_count, width), low),
            shape((shards, slot_count // shards, width), low), shape((4, width, width), low),
            shape((keys, width), low), shape((width, TILE), low),
            shape((width, keys), low), shape((rows, width), low), shape((keys, width), low),
            shape((keys, width), low), shape((width, rows), single), shape((rows, width), single),
        ),
        in_specs=[in_vmem] * 3 + [anywhere] * 6,
        out_specs=(in_vmem,) * 6 + (anywhere,) * 10,
        scratch_shapes=[
            vm((2, tile_kinds, TILE, TILE), single), vm((TILE, keys), low), vm((keys - 2 * SPAN, 2 * rows), single),
            vm((2 * SPAN, 2 * (rows - TILE)), single),
            vm((shards, slot_count // shards, width), low), vm((4, width, width), low), vm((keys, width), low),
            vm((width, TILE), low), vm((rows, width), low), vm((4, lines, width), low), vm((lines, TILE), low),
            vm((keys, width), low), vm((width, keys), low), vm((rows, width), low), vm((keys, width), low),
            vm((keys, width), low), vm((width, rows), single), vm((rows, width), single),
            sem((shards - 1,)), sem((shards - 1,)), sem((16,)), sem((count,)), sem((count,)), sem((count,)),
            sem((count,)), sem((count,)), sem((count,)), sem((count, 3)), sem((count, 3)), sem((chips,)), sem((chips,)),
            sem((chips,)), sem((chips,)), sem((chips,)), sem((chips,)), sem((1,)), sem((1,)),
        ],
        compiler_params=pltpu.CompilerParams(collective_id=2, has_side_effects=True, vmem_limit_bytes=vmem_cap),
        cost_estimate=pl.CostEstimate(flops=30_000_000_000, bytes_accessed=20_000_000, transcendentals=8_000_000),
        name="front",
    )(ints, bucket_row, cotangent, *weights, tokens, small)


def moe_kernel(
    x_ref, g_ref, small_ref, w_in_ref, w_out_ref,
    back_ref, out_ref, gwin_ref, gwout_ref, rg_ref,
    w_in, w_out, xin, gm, gg, hid, gpre, logit_grads, x_t, gwin, gwout,
    xs, xr, ms, mr, ws, ls, os_in, os_out,
):
    rep, chip, core, chips, quarter = places()
    experts = chips * 2
    here = chip * 2 + core
    pair_rows = 2 * xin.shape[2]
    hidden = w_in_ref.shape[1]
    block = BLOCK
    loads = [
        pltpu.make_async_copy(w_in_ref, w_in, ws.at[0]),
        pltpu.make_async_copy(w_out_ref, w_out, ws.at[1]),
    ]
    for copy in loads:
        copy.start()
    twin = (rep, chip * 2 + 1 - core)
    targets = [
        (k, side, (rep, chip_across(chip, k) * 2 + side)) for k in range(1, chips) for side in range(2)
    ]
    greet([twin] + [device for _, _, device in targets])
    sent = [send(x_ref.at[chip, 1 - core], xin.at[chip, core], (xs.at[0, 0], xr.at[0, core]), twin)]
    for k, side, device in targets:
        sent.append(
            send(x_ref.at[chip_across(chip, k), side], xin.at[chip, core], (xs.at[k, side], xr.at[k, core]), device)
        )
    for copy in sent[:5]:
        copy.start()
    xin[chip, core] = x_ref[chip, core]
    for copy in loads:
        copy.wait()

    def arrived(k, source, side):
        piece = xin.at[source, side]
        send(piece, piece, (xs.at[0, 0], xr.at[k, side]), twin).wait_recv()

    @pl.loop(0, chips)
    def chunk(k):
        source = chip_across(chip, k)

        @pl.when(k == 0)
        def _():
            arrived(0, chip, 1 - core)

        @pl.when(k > 0)
        def _():
            for side in range(2):
                arrived(k, source, side)

        rows = xin[source].reshape(pair_rows, xin.shape[3])
        grads = g_ref[source].reshape(pair_rows, xin.shape[3])
        probs = router_softmax(rows, small_ref[...], experts)
        lanes = lax.broadcasted_iota(jnp.int32, probs.shape, 1)
        gate = jnp.sum(jnp.where(lanes == here, probs, 0.0), axis=1, keepdims=True)
        gated = (gate * grads.astype(single)).astype(low)
        span = pl.ds(pl.multiple_of(source * pair_rows, pair_rows), pair_rows)
        gg[span, :] = gated
        pre = nn(rows, w_in[...])
        grad_hidden = nt(gated, w_out[...])
        square = pre * pre
        wave = jnp.tanh(0.7978845608028654 * pre * (1.0 + 0.044715 * square))
        left = 0.5 + 0.5 * wave
        active = (pre * left).astype(low)
        slope = left + (0.5 * pre) * (1.0 - wave * wave) * (0.7978845608028654 + 0.10703222440890037 * square)
        grad_pre = (grad_hidden * slope).astype(low)
        hid[span, :] = active
        gpre[span, :] = grad_pre
        out = nn(active, w_out[...]).astype(low)
        out_ref[source] = out.reshape(out_ref.shape[1:])
        grad_gate = jnp.sum(grads.astype(single) * out.astype(single), axis=1, keepdims=True)
        chosen = jnp.where(lanes == here, 1.0, 0.0)
        grad_logits = jnp.where(lanes < experts, gate * grad_gate * (chosen - probs), 0.0)
        logit_grads[span, :] = grad_logits
        router = small_ref[...]
        total = nt(grad_pre, w_in[...]) + sum(nt(part, router) for part in thirds_of(grad_logits))
        gm[source] = total.astype(low).reshape(gm.shape[1:])

        def reply(side, slot):
            return send(
                gm.at[source, side], back_ref.at[chip, core], (ms.at[k, slot], mr.at[k, core]), (rep, source * 2 + side)
            )

        @pl.when(k == 0)
        def _():
            for copy in sent[5:]:
                copy.start()
            reply(1 - core, 0).start()
            pltpu.make_async_copy(gm.at[chip, core], back_ref.at[chip, core], ls).start()

        @pl.when(k > 0)
        def _():
            for side in range(2):
                reply(side, side).start()

    every = xin[...].reshape(gg.shape)
    x_t[...] = every.T

    def strip_writes(part):
        cols = pl.ds(pl.multiple_of(part * block, block), block)
        return [
            pltpu.make_async_copy(gwin.at[:, cols], gwin_ref.at[:, cols], os_in.at[part]),
            pltpu.make_async_copy(gwout.at[cols], gwout_ref.at[cols], os_out.at[part]),
        ]

    @pl.loop(0, hidden // block)
    def strip(part):
        cols = pl.ds(pl.multiple_of(part * block, block), block)
        first, second = strip_writes(part)
        gwin[:, cols] = nn(x_t[...], gpre[:, cols]).astype(low)
        first.start()
        gwout[cols, :] = tn(hid[:, cols], gg[...]).astype(low)
        second.start()

    rg_ref[...] = sum(nn(x_t[...], part) for part in thirds_of(logit_grads[...]))
    pltpu.make_async_copy(gm.at[chip, core], back_ref.at[chip, core], ls).wait()

    def replied(k, source, side):
        piece = back_ref.at[source, side]
        send(piece, piece, (ms.at[0, 0], mr.at[k, side]), twin).wait_recv()

    replied(0, chip, 1 - core)
    for k in range(1, chips):
        for side in range(2):
            replied(k, chip_across(chip, k), side)
    for copy in sent:
        copy.wait_send()
    for part in range(hidden // block):
        for copy in strip_writes(part):
            copy.wait()
    send(gm.at[chip, 0], back_ref.at[chip, core], (ms.at[0, 0], mr.at[0, 0]), twin).wait_send()
    for k in range(1, chips):
        for side in range(2):
            send(gm.at[chip, 0], back_ref.at[chip, core], (ms.at[k, side], mr.at[0, 0]), twin).wait_send()


def moe(rows_out, grad_in, small, w_in, w_out):
    chips, _, cap, width = rows_out.shape
    slots = chips * 2 * cap
    hidden = w_in.shape[1]
    shape = jax.ShapeDtypeStruct
    pairs = pltpu.SemaphoreType.DMA
    strips = hidden // BLOCK
    return pl.pallas_call(
        moe_kernel,
        out_shape=(
            shape(rows_out.shape, low), shape(rows_out.shape, low), shape((width, hidden), low),
            shape((hidden, width), low), shape((width, TILE), single),
        ),
        in_specs=[in_vmem] * 3 + [anywhere] * 2,
        out_specs=(anywhere, in_vmem, anywhere, anywhere, in_vmem),
        scratch_shapes=[
            pltpu.VMEM((width, hidden), low), pltpu.VMEM((hidden, width), low),
            pltpu.VMEM(rows_out.shape, low), pltpu.VMEM(rows_out.shape, low), pltpu.VMEM((slots, width), low),
            pltpu.VMEM((slots, hidden), low), pltpu.VMEM((slots, hidden), low),
            pltpu.VMEM((slots, TILE), single), pltpu.VMEM((width, slots), low), pltpu.VMEM((width, hidden), low), pltpu.VMEM((hidden, width), low),
            pairs((chips, 2)), pairs((chips, 2)), pairs((chips, 2)), pairs((chips, 2)), pairs((2,)), pairs,
            pairs((strips,)), pairs((strips,)),
        ],
        compiler_params=pltpu.CompilerParams(collective_id=3, has_side_effects=True, vmem_limit_bytes=vmem_cap),
        cost_estimate=pl.CostEstimate(flops=40_000_000_000, bytes_accessed=40_000_000, transcendentals=3_000_000),
        name="moe",
    )(rows_out, grad_in, small, w_in, w_out)


def back_kernel(
    col_ref, gain_ref, lse_ref, rev_ref, bucket_ref, rg_ref, back_hbm, mid_hbm, cot_hbm, q_hbm, k_hbm, v_hbm, o_hbm,
    every_hbm, w_hbm, n_hbm, gwin_hbm, gwout_hbm, out_hbm,
    z_ref, dense_hbm, p_hbm, e_hbm, own_hbm, gres_hbm, ra_hbm, rb_hbm, ret_hbm,
    tiles, sums, diag, kt, dqt, far_sums, g_ref, dq_ref, dk_ref, dv_ref, attn_gain,
    every_ref, w_ref, n_ref, back_ref, mid_ref, cot_ref, q_ref, k_ref, v_ref, o_ref,
    dense_ref, own_ref, gres_ref,
    o_grad, o_half, o_sum, o_in, h_grad, h_half, h_sum, h_in,
    loc, out, xs, xr, as_, ar, bs, br, os_, or_, oz_s, oz_r, hs_, hr_, hz_s, hz_r,
):
    shard_id = lax.axis_index("shard")
    shards = lax.axis_size("shard")
    rows, width = mid_ref.shape
    blocks = k_ref.shape[0] // TILE - 4
    half = TILE // 2
    experts = shards
    heads_held = rev_ref.shape[0]
    rep, slow, fast, slows, fasts = rep_places()
    _, chip, core, chips, _ = places()
    along, _, twin = peer_lists()
    loads = [
        pltpu.make_async_copy(source, target, loc.at[i])
        for i, (source, target) in enumerate((
            (back_hbm, back_ref), (mid_hbm, mid_ref), (cot_hbm, cot_ref), (w_hbm.at[3], w_ref.at[3]), (o_hbm, o_ref),
            (q_hbm, q_ref), (k_hbm, k_ref), (v_hbm, v_ref), (n_hbm, n_ref), (w_hbm.at[pl.ds(0, 3)], w_ref.at[pl.ds(0, 3)]),
            (every_hbm, every_ref), (out_hbm.at[chip, core], ret_hbm.at[chip, core]),
        ))
    ]
    for copy in loads:
        copy.start()
    writes = []

    def write(source, target):
        writes.append(pltpu.make_async_copy(source, target, out.at[len(writes)]))
        writes[-1].start()

    beside = [(slow * fasts + (fast + j) % fasts, shard_id) for j in range(1, fasts)]
    beyond = [((slow + j) % slows * fasts + fast, shard_id) for j in range(1, slows)]
    nearby = result_peers(rep, chip, core, range(NEAR))
    far_twins = [(rep, (chip + k) % chips * 2 + 1 - core) for k in range(1, chips)]
    greet([twin] + along + far_twins + beside + beyond)
    sent = [
        send(gwin_hbm.at[:, (fast + j + 1) % fasts], ra_hbm.at[j], (as_.at[j], ar.at[j]), device)
        for j, device in enumerate(beside)
    ] + [
        send(gwout_hbm.at[(slow + j + 1) % slows], rb_hbm.at[j], (bs.at[j], br.at[j]), device)
        for j, device in enumerate(beyond)
    ] + [
        send(out_hbm.at[chip_across(chip, k), side if k else 1 - core], ret_hbm.at[chip, core], (xs.at[k, side], xr.at[k, core]), device)
        for k, side, device in nearby
    ]
    for copy in sent:
        copy.start()
    diag[...] = jnp.zeros_like(diag)
    far_sums[...] = jnp.zeros_like(far_sums)
    tile_rows = lax.broadcasted_iota(jnp.int32, (TILE, TILE), 0)
    tile_cols = lax.broadcasted_iota(jnp.int32, (TILE, TILE), 1)
    flip = (tile_rows + tile_cols == TILE - 1).astype(single)

    for copy in loads[:5]:
        copy.wait()
    slots = lax.broadcasted_iota(jnp.int32, (rows, back_ref.shape[0]), 1)
    grad_mid = nn((slots == col_ref[:, 0:1]).astype(low), back_ref[...])
    resid_mid = mid_ref[...]
    grad_gain_moe = jnp.sum(grad_mid * resid_mid * inverse_rms(resid_mid), axis=0, keepdims=True)
    grad_resid = cot_ref[...].astype(single) + norm_pull(grad_mid, resid_mid, gain_ref[1:2, :])
    gres_ref[...] = grad_resid
    write(gres_ref, gres_hbm)
    grad_attn = grad_resid.astype(low)
    g_ref[...] = nt(grad_attn, w_ref[3]).astype(low)
    o_grad[...] = nn(o_ref[...].astype(low), grad_attn).reshape(o_grad.shape).astype(low)
    o_halves = [send(o_grad.at[2 * k + 1 - core], o_half.at[k], (os_.at[k], or_.at[k]), twin) for k in range(chips)]
    o_sends = [
        send(o_sum.at[(chip + k + 1) % chips], o_in.at[k], (oz_s.at[k], oz_r.at[k]), device)
        for k, device in enumerate(along)
    ]
    for copy in o_halves:
        copy.start()
    h_halves = [send(h_grad.at[2 * k + 1 - core], h_half.at[k], (hs_.at[k], hr_.at[k]), twin) for k in range(chips)]
    h_sends = [
        send(h_sum.at[(chip + k + 1) % chips], h_in.at[k], (hz_s.at[k], hz_r.at[k]), device)
        for k, device in enumerate(along)
    ]
    for copy in loads[5:]:
        copy.wait()
    own = pl.ds(pl.multiple_of(shard_id * TILE, TILE), TILE)
    tail = slice((blocks + 2) * TILE, (blocks + 4) * TILE)
    early = width // 2

    @pl.loop(0, width // TILE)
    def pair_loop(pair):
        cols = pl.ds(pl.multiple_of(pair * TILE, TILE), TILE)
        kt[...] = k_ref[:, cols].T
        g_pair = g_ref[:, cols]
        q_both, g_both = both_heads(q_ref[:, cols]), both_heads(g_pair)
        delta_t = g_pair.astype(single).T * o_ref[cols, :]
        delta = jnp.concatenate(
            [jnp.sum(delta_t[:half], axis=0, keepdims=True), jnp.sum(delta_t[half:], axis=0, keepdims=True)], axis=1
        )
        log_total = jnp.concatenate([lse_ref[pl.ds(pair * 2, 1), :], lse_ref[pl.ds(pair * 2 + 1, 1), :]], axis=1)
        for side in range(2):
            rev_row = rev_ref[pl.ds(pair * 2 + side, 1), :]
            fill_tiles(tiles.at[side], rev_row, rev_row[:, SPAN - 1 : SPAN], rev_row[:, SPAN : SPAN + 1])
        sums[...] = jnp.zeros_like(sums)

        def block_grads(part, q_rows, g_rows, shift, scale, grid):
            keys = slice(part * SPAN, (part + 1) * SPAN)
            count = q_rows.shape[0] // 2
            scores = with_bias(nt(k_ref[keys, cols], q_rows), tiles, grid)
            weights = jnp.exp(scores - shift)
            grad_scores = weights * (nt(v_ref[keys, cols], g_rows) - scale)
            for i, row in enumerate(grid):
                for j, (side, kind) in enumerate(row):
                    sums[side, kind] += tile_of(grad_scores, i, j)
            raw = grad_scores.astype(low)
            dk_ref[keys, cols] = nn(raw, q_rows).astype(low)
            dv_ref[keys, cols] = nn(weights.astype(low), g_rows).astype(low)
            return [nn(kt[:half, keys], raw[:, :count]), nn(kt[half:, keys], raw[:, count:])]

        grads = [jnp.zeros((half, rows), single)] * 2
        for part in range(blocks // 2):
            more = block_grads(part, q_both, g_both, log_total, delta, prompt_grid(part, shard_id, blocks))
            grads = [old + new for old, new in zip(grads, more)]
        local = [old[:, PR_DEV:] for old in grads]
        held = (continuation(q_both, 0), continuation(g_both, 0), continuation(log_total, 1), continuation(delta, 1))
        for part in range(2):
            more = block_grads(blocks // 2 + part, *held, local_grid(part, shard_id))
            local = [old + new for old, new in zip(local, more)]
        for side in range(2):
            head = pair * 2 + side
            dqt[side * half : (side + 1) * half, :] = jnp.concatenate([grads[side][:, :PR_DEV], local[side]], axis=1)
            near = jnp.concatenate(
                [
                    sums[side, 1] + sums[side, causal_tile], sums[side, 0], jnp.zeros((TILE, TILE), single),
                    sums[side, 2],
                ],
                axis=1,
            )
            flipped = jnp.dot(flip, near, precision=lax.Precision.HIGHEST, preferred_element_type=single)
            rolled = pltpu.roll(flipped, 3 * TILE + 1, 1, stride=1, stride_axis=0)
            diag[pl.ds(head, 1), :] = jnp.sum(rolled, axis=0, keepdims=True)
            far_sums[pl.ds(head, 1), :] = jnp.concatenate(
                [
                    jnp.sum(sums[side, far_before], axis=0, keepdims=True),
                    jnp.sum(sums[side, far_after], axis=0, keepdims=True),
                ],
                axis=1,
            )
        dq_ref[:, cols] = (dqt[...].T * 0.125).astype(low)

        @pl.when(pair == 0)
        def _():
            for k in range(chips):
                o_halves[k].wait_recv()
                o_sum[k] = (o_grad[2 * k + core].astype(single) + o_half[k].astype(single)).astype(low)
            for copy in o_sends:
                copy.start()

        @pl.when(pair == width // SPAN - 1)
        def _():
            normed = jnp.concatenate([n_ref[:, own], n_ref[:, tail]], axis=1)
            for i, (left, right) in enumerate(((normed, dq_ref), (n_ref[...], dk_ref), (n_ref[...], dv_ref))):
                part = nn(left, right[:, :early]).reshape(shards, h_grad.shape[1], early)
                h_grad[:, :, i * early : (i + 1) * early] = part.astype(low)
            for copy in h_halves:
                copy.start()

        @pl.when(pair == width // SPAN)
        def _():
            for k in range(chips):
                h_halves[k].wait_recv()
                h_sum[k] = (h_grad[2 * k + core].astype(single) + h_half[k].astype(single)).astype(low)
            for copy in h_sends:
                copy.start()

    lanes = lax.broadcasted_iota(jnp.int32, (heads_held, 4 * TILE), 1)
    before = jnp.sum(far_sums[:, :TILE], axis=1, keepdims=True)
    after = jnp.sum(far_sums[:, TILE:], axis=1, keepdims=True)
    by_gap = diag[...] + jnp.where(lanes == SPAN - 1, before, 0.0) + jnp.where(lanes == SPAN, after, 0.0)
    shard_rows = width // shards
    table_rows = 2 * TILE // 8 // shards
    owner = lax.broadcasted_iota(jnp.int32, (shards, shard_rows, 4 * TILE), 0)
    offset = lax.broadcasted_iota(jnp.int32, (shards, shard_rows, 4 * TILE), 1)
    held = jnp.where(offset < table_rows, owner * table_rows + offset, -1).reshape(width, 4 * TILE)
    hot = (held == bucket_ref[0:1, :]).astype(low)
    grad_table = sum(nt(part, hot) for part in thirds_of(by_gap))

    attn_gain[...] = jnp.zeros_like(attn_gain)
    normed = jnp.concatenate([n_ref[:, own], n_ref[:, tail]], axis=1)
    dense_ref[:, :early] = nn(normed, dq_ref[:, early:]).astype(low)
    grad_own = nt(dq_ref[...], w_ref[0])
    values = jnp.concatenate([every_ref[own, :], every_ref[tail, :]], axis=0).astype(single)
    attn_gain[...] += jnp.sum(fold8(grad_own * (values * inverse_rms(values))), axis=0)
    own_ref[...] = grad_own

    def pull_rows(part):
        span = pl.ds(pl.multiple_of(part * SPAN, SPAN), SPAN)
        values = every_ref[span, :].astype(single)
        grads = nt(dk_ref[span, :], w_ref[1]) + nt(dv_ref[span, :], w_ref[2])
        attn_gain[...] += jnp.sum(fold8(grads * (values * inverse_rms(values))), axis=0)
        return grads

    @pl.loop(0, blocks // 2)
    def pull_prompt(part):
        k_ref[pl.ds(pl.multiple_of(part * SPAN, SPAN), SPAN), :] = pull_rows(part).astype(low)

    write(k_ref.at[pl.ds(0, blocks * TILE)], p_hbm)
    k_ref[blocks * TILE : (blocks + 2) * TILE, :] = pull_rows(blocks // 2).astype(low)
    write(k_ref.at[pl.ds(blocks * TILE, SPAN)], e_hbm)
    own_ref[PR_DEV:, :] += pull_rows(blocks // 2 + 1)
    write(own_ref, own_hbm)

    dense_ref[:, early : 2 * early] = nn(n_ref[...], dk_ref[:, early:]).astype(low)
    dense_ref[:, 2 * early : 3 * early] = nn(n_ref[...], dv_ref[:, early:]).astype(low)

    small_t = jnp.concatenate(
        [
            jnp.zeros((experts, width), single), jnp.sum(attn_gain[...], axis=0, keepdims=True), grad_gain_moe,
            grad_table, jnp.zeros((TILE - experts - 2 - heads_held, width), single),
        ],
        axis=0,
    )
    dense_ref[:, 3 * early :] = (small_t.T + rg_ref[...]).astype(low)
    write(dense_ref, dense_hbm)
    o_total = o_sum[chip].astype(single)
    for k in range(chips - 1):
        o_sends[k].wait_recv()
        o_total = o_total + o_in[k].astype(single)
    z_ref[:, :width] = o_total.astype(low)
    h_total = h_sum[chip].astype(single)
    for k in range(chips - 1):
        h_sends[k].wait_recv()
        h_total = h_total + h_in[k].astype(single)
    z_ref[:, width:] = h_total.astype(low)
    for copy in o_halves + o_sends + h_halves + h_sends:
        copy.wait_send()
    for copy in writes:
        copy.wait()
    for k, side in result_slots(core, range(NEAR)):
        piece = ret_hbm.at[chip_across(chip, k), side]
        send(piece, piece, (xs.at[0, 0], xr.at[k, side]), twin).wait_recv()
    for j in range(fasts - 1):
        send(ra_hbm.at[j], ra_hbm.at[j], (as_.at[j], ar.at[j]), twin).wait_recv()
    for j in range(slows - 1):
        send(rb_hbm.at[j], rb_hbm.at[j], (bs.at[j], br.at[j]), twin).wait_recv()
    for copy in sent:
        copy.wait_send()


def back(
    returned, col_slots, mid, cotangent, gains, every_tok, weights, kept, bucket_row, router_grads, gwin, gwout, result
):
    rows, width = mid.shape
    normed, queries, keys, values, attended, lse, rev = kept
    count = keys.shape[0]
    shards = lax.axis_size("shard")
    slows, fasts = gwin.shape[:2]
    chips, lines, early = shards // 2, width // shards, width // 2
    vm = pltpu.VMEM
    shape = jax.ShapeDtypeStruct
    pairs = pltpu.SemaphoreType.DMA
    args = (
        col_slots, gains, lse, rev, bucket_row, router_grads, returned, mid, cotangent, queries, keys, values, attended,
        every_tok, weights, normed, gwin, gwout, result,
    )
    return pl.pallas_call(
        back_kernel,
        out_shape=(
            shape((lines, width + 3 * early), low), shape((width, 3 * early + TILE), low),
            shape((count - 2 * SPAN, width), low), shape((SPAN, width), low),
            shape((rows, width), single), shape((rows, width), single),
            shape((fasts - 1, slows) + gwin.shape[2:], low), shape((slows - 1, fasts) + gwout.shape[2:], low),
            shape(result.shape, low),
        ),
        in_specs=[in_vmem] * 6 + [anywhere] * 13,
        out_specs=(in_vmem,) + (anywhere,) * 8,
        scratch_shapes=[
            pltpu.VMEM((2, tile_kinds, TILE, TILE), single), pltpu.VMEM((2, tile_kinds, TILE, TILE), single),
            pltpu.VMEM((16, 4 * TILE), single), pltpu.VMEM((TILE, count), low), pltpu.VMEM((TILE, rows), single),
            pltpu.VMEM((16, 2 * TILE), single),
            pltpu.VMEM((rows, width), low), pltpu.VMEM((rows, width), low), pltpu.VMEM((count, width), low),
            pltpu.VMEM((count, width), low), pltpu.VMEM((8, width), single),
            pltpu.VMEM(every_tok.shape, low), pltpu.VMEM(weights.shape, low), pltpu.VMEM(normed.shape, low),
            vm(returned.shape, low), vm((rows, width), single), vm((rows, width), low), vm((rows, width), low),
            vm(keys.shape, low), vm(keys.shape, low), vm(attended.shape, single),
            vm((width, 3 * early + TILE), low),
            vm((rows, width), single), vm((rows, width), single),
            vm((shards, lines, width), low), vm((chips, lines, width), low),
            vm((chips, lines, width), low), vm((chips - 1, lines, width), low),
            vm((shards, lines, 3 * early), low), vm((chips, lines, 3 * early), low),
            vm((chips, lines, 3 * early), low), vm((chips - 1, lines, 3 * early), low),
            pairs((12,)), pairs((6,)), pairs((NEAR, 2)), pairs((NEAR, 2)), pairs((fasts - 1,)), pairs((fasts - 1,)),
            pairs((slows - 1,)), pairs((slows - 1,)), pairs((chips,)), pairs((chips,)), pairs((chips - 1,)),
            pairs((chips - 1,)), pairs((chips,)), pairs((chips,)), pairs((chips - 1,)), pairs((chips - 1,)),
        ],
        compiler_params=pltpu.CompilerParams(collective_id=4, has_side_effects=True, vmem_limit_bytes=vmem_cap),
        cost_estimate=pl.CostEstimate(flops=60_000_000_000, bytes_accessed=40_000_000, transcendentals=8_000_000),
        name="back",
    )(*args)


def places():
    rep, shard = lax.axis_index("rep"), lax.axis_index("shard")
    return rep, shard // 2, shard % 2, lax.axis_size("shard") // 2, rep % QUARTERS


def peer_lists():
    rep, chip, core, chips, quarter = places()
    along = [(rep, (chip + k) % chips * 2 + core) for k in range(1, chips)]
    across = [(rep - quarter + (quarter + j) % QUARTERS, chip * 2 + core) for j in range(1, QUARTERS)]
    twin = (rep, chip * 2 + 1 - core)
    return along, across, twin


def chip_across(chip, k):
    partner, bit = 0, 1
    while bit < lax.axis_size("shard") // 2:
        partner = partner + bit * ((chip // bit + k // bit) % 2)
        bit = bit * 2
    return partner


def result_peers(rep, chip, core, chosen):
    return [
        (k, side, (rep, chip_across(chip, k) * 2 + (side if k else 1 - core)))
        for k in chosen for side in range(2 if k else 1)
    ]


def result_slots(core, chosen):
    return [(k, side if k else 1 - core) for k in chosen for side in range(2 if k else 1)]


def greet(devices):
    barrier = pltpu.get_barrier_semaphore()
    for device in devices:
        pl.semaphore_signal(barrier, inc=1, device_id=device, device_id_type=mesh_ids)
    pl.semaphore_wait(barrier, len(devices))


def send(source, target, sems, device):
    return pltpu.make_async_remote_copy(
        src_ref=source, dst_ref=target, send_sem=sems[0], recv_sem=sems[1],
        device_id=device, device_id_type=mesh_ids,
    )


def rep_places():
    rep, reps = lax.axis_index("rep"), lax.axis_size("rep")
    fasts = QUARTERS if reps % (QUARTERS * QUARTERS) == 0 else 2
    return rep, rep // fasts, rep % fasts, reps // fasts, fasts


def reduce_kernel(
    gain_ref, col_ref, d_hbm, p_hbm, e_hbm, own_hbm, gres_hbm, tok_hbm, mid_hbm, gate_hbm, out_hbm, ret_hbm,
    gwin_hbm, ra_hbm, gwout_hbm, rb_hbm, z_hbm,
    gt_ref, mix_ref, early_ref, late_ref, ka_ref, la_hbm, kb_ref, lb_hbm,
    d_own, half, hr, tr, mr, cr, zs, tz, z_last, z_above, z_all, last, above_in, gathered,
    p_own, p_half, p_sum, p_in, e_in, own, gres, tok, mid, gate, ret,
    a_own, a_in, a_sum, b_own, b_in, b_sum,
    loc, ps_s, ps_r, ds_s, ds_r, pz_s, pz_r, rr_s, rr_r, rz_s, rz_r, zr_s, zr_r, zh_s, zh_r, za_s, za_r,
    dh_s, dh_r, da_s, da_r, ea_s, ea_r, eb_s, eb_r, xs, xr,
):
    rep, chip, core, chips, quarter = places()
    along, across, twin = peer_lists()
    _, slow, fast, slows, fasts = rep_places()
    classes = lax.axis_size("rep") // QUARTERS
    here = chip * 2 + core
    beside = [(slow * fasts + (fast + j) % fasts, here) for j in range(1, fasts)]
    beyond = [((slow + j) % slows * fasts + fast, here) for j in range(1, slows)]
    above = [((rep // QUARTERS + k) % classes * QUARTERS + quarter, here) for k in range(1, classes)]
    wide = lambda held: held.astype(single)
    pending = []

    def load(source, target, index):
        copy = pltpu.make_async_copy(source, target, loc.at[index])
        copy.start()
        return copy

    def go(source, target, sems, device):
        copy = send(source, target, sems, device)
        copy.start()
        pending.append(copy)

    def landed(piece, sems):
        send(piece, piece, sems, twin).wait_recv()

    early_in = load(z_hbm, zs, 12)
    a_loads = [load(gwin_hbm.at[:, fast], a_own, 0), load(ra_hbm, a_in, 1)]
    halves = [load(d_hbm.at[:, core], d_own, 5), load(p_hbm.at[:, core], p_own, 4)]
    b_loads = [load(gwout_hbm.at[slow], b_own, 2), load(rb_hbm, b_in, 3)]
    rest = [
        load(ret_hbm.at[chip_across(chip, k)], ret.at[chip_across(chip, k)], 13 + k) for k in range(NEAR)
    ] + [
        load(mid_hbm, mid, 7), load(gate_hbm, gate, 8), load(own_hbm, own, 9),
        load(gres_hbm, gres, 10), load(tok_hbm, tok, 11),
    ]
    others = [(rep, (here + k) % (2 * chips)) for k in range(1, 2 * chips)]
    greets = list(others)
    for device in across + beside + beyond + above:
        greets.append(device)
    greet(greets)
    for k in range(chips):
        go(d_hbm.at[k, 1 - core], half.at[k], (ds_s.at[k], ds_r.at[k]), twin)
    go(p_hbm.at[:, 1 - core], p_half, (ps_s.at[0], ps_r.at[0]), twin)
    go(e_hbm, e_in, (ps_s.at[1], ps_r.at[1]), twin)
    for k, side, device in result_peers(rep, chip, core, range(NEAR, chips)):
        go(out_hbm.at[chip_across(chip, k), side], ret.at[chip, core], (xs.at[k - NEAR, side], xr.at[k - NEAR, core]), device)
    early_in.wait()
    for j, device in enumerate(across):
        go(zs.at[(quarter + j + 1) % QUARTERS], tz.at[j], (zr_s.at[j], zr_r.at[j]), device)

    for copy in a_loads:
        copy.wait()
    for t in range(slows):
        total = wide(a_own[t])
        for j in range(fasts - 1):
            total = total + wide(a_in[j, t])
        a_sum[t] = total.astype(low)
    for j, device in enumerate(beyond):
        go(a_sum.at[(slow + j + 1) % slows], la_hbm.at[j], (ea_s.at[j], ea_r.at[j]), device)
    for copy in halves:
        copy.wait()
    for k in range(chips):
        landed(half.at[k], (ds_s.at[k], ds_r.at[k]))
        for t in range(QUARTERS):
            hr[t, k] = (wide(d_own[k, t]) + wide(half[k, t])).astype(low)
    for j, device in enumerate(across):
        go(hr.at[(quarter + j + 1) % QUARTERS], tr.at[j], (rr_s.at[j], rr_r.at[j]), device)
    landed(p_half, (ps_s.at[0], ps_r.at[0]))
    for k in range(chips):
        p_sum[k] = (wide(p_own[k]) + wide(p_half[k])).astype(low)
    for k, device in enumerate(along):
        go(p_sum.at[(chip + k + 1) % chips], p_in.at[k], (pz_s.at[k], pz_r.at[k]), device)
    for copy in b_loads:
        copy.wait()
    for t in range(fasts):
        total = wide(b_own[t])
        for j in range(slows - 1):
            total = total + wide(b_in[j, t])
        b_sum[t] = total.astype(low)
    for j, device in enumerate(beside):
        go(b_sum.at[(fast + j + 1) % fasts], lb_hbm.at[j], (eb_s.at[j], eb_r.at[j]), device)

    def class_sum(held, came, s_sems, r_sems):
        total = wide(held[...])
        for j, device in enumerate(above):
            go(held, came.at[j], (s_sems.at[j], r_sems.at[j]), device)
        for j in range(classes - 1):
            landed(came.at[j], (s_sems.at[j], r_sems.at[j]))
            total = total + wide(came[j])
        return total.astype(low)

    def hand_out(pieces, s_sems, r_sems):
        for j, device in enumerate(across):
            go(pieces.at[quarter], pieces.at[quarter], (s_sems.at[j], r_sems.at[j]), device)

    def handed(pieces, s_sems, r_sems):
        for j in range(QUARTERS - 1):
            landed(pieces.at[(quarter + QUARTERS - j - 1) % QUARTERS], (s_sems.at[j], r_sems.at[j]))

    for j in range(QUARTERS - 1):
        landed(tz.at[j], (zr_s.at[j], zr_r.at[j]))
    total = wide(zs[quarter])
    for j in range(QUARTERS - 1):
        total = total + wide(tz[j])
    z_last[...] = total.astype(low)
    z_all[quarter] = class_sum(z_last, z_above, zh_s, zh_r) if classes > 1 else z_last[...]
    hand_out(z_all, za_s, za_r)

    for copy in rest:
        copy.wait()
    ka_ref[...] = a_sum[slow]
    kb_ref[...] = b_sum[fast]

    for j in range(QUARTERS - 1):
        landed(tr.at[j], (rr_s.at[j], rr_r.at[j]))
    for k in range(chips):
        total = wide(hr[quarter, k])
        for j in range(QUARTERS - 1):
            total = total + wide(tr[j, k])
        mr[k] = total.astype(low)
    for k, device in enumerate(along):
        go(mr.at[(chip + k + 1) % chips], cr.at[k], (rz_s.at[k], rz_r.at[k]), device)

    for k in range(chips - 1):
        landed(p_in.at[k], (pz_s.at[k], pz_r.at[k]))
    landed(e_in, (ps_s.at[1], ps_r.at[1]))
    total = wide(p_sum[chip])
    for k in range(chips - 1):
        total = total + wide(p_in[k])
    grads = own[...] + jnp.concatenate([total, wide(e_in[...])], axis=0)
    gt_ref[...] = gres[...] + norm_pull(grads, wide(tok[...]), gain_ref[0:1, :])

    for k in range(chips - 1):
        landed(cr.at[k], (rz_s.at[k], rz_r.at[k]))
    total = wide(mr[chip])
    for k in range(chips - 1):
        total = total + wide(cr[k])
    last[...] = total.astype(low)
    gathered[quarter] = class_sum(last, above_in, dh_s, dh_r) if classes > 1 else last[...]
    hand_out(gathered, da_s, da_r)
    for k, side in result_slots(core, range(NEAR, chips)):
        landed(ret.at[chip_across(chip, k), side], (xs.at[k - NEAR, side], xr.at[k - NEAR, side]))
    slots = lax.broadcasted_iota(jnp.int32, (tok.shape[0], 2 * chips * ret.shape[2]), 1)
    chosen = nn((slots == col_ref[:, 0:1]).astype(low), ret[...].reshape(slots.shape[1], tok.shape[1]))
    mix_ref[...] = (mid[...] + gate[:, 0:1] * chosen).astype(low)
    handed(z_all, za_s, za_r)
    early_ref[...] = z_all[...]
    handed(gathered, da_s, da_r)
    late_ref[...] = gathered[...]
    for j in range(slows - 1):
        landed(la_hbm.at[j], (ea_s.at[j], ea_r.at[j]))
    for j in range(fasts - 1):
        landed(lb_hbm.at[j], (eb_s.at[j], eb_r.at[j]))
    for copy in pending:
        copy.wait_send()


def reduce_all(gains, col_slots, dense, prompt_part, near_part, own, gres, tokens, mid, gate, result, returned, gwin, ra, gwout, rb, z):
    chips = lax.axis_size("shard") // 2
    classes = lax.axis_size("rep") // QUARTERS
    slows, fasts = gwin.shape[:2]
    rows, width = mid.shape
    lines, lanes = dense.shape[3:]
    wider = z.shape[2]
    shape = jax.ShapeDtypeStruct
    sem = pltpu.SemaphoreType.DMA
    vm = pltpu.VMEM
    count, others = chips - 1, QUARTERS - 1
    ours = prompt_part.shape[2:]
    extra = max(classes - 1, 1)
    args = (gains, col_slots, dense, prompt_part, near_part, own, gres, tokens, mid, gate, result, returned, gwin, ra, gwout, rb, z)
    return pl.pallas_call(
        reduce_kernel,
        out_shape=(
            shape((rows, width), single), shape((rows, width), low),
            shape((QUARTERS, lines, wider), low), shape((QUARTERS, lines, lanes), low),
            shape(gwin.shape[2:], low), shape((slows - 1,) + gwin.shape[2:], low),
            shape(gwout.shape[2:], low), shape((fasts - 1,) + gwout.shape[2:], low),
        ),
        in_specs=[in_vmem] * 2 + [anywhere] * 15,
        out_specs=(in_vmem,) * 5 + (anywhere, in_vmem, anywhere),
        scratch_shapes=[
            vm((chips, QUARTERS, lines, lanes), low), vm((chips, QUARTERS, lines, lanes), low),
            vm((QUARTERS, chips, lines, lanes), low), vm((others, chips, lines, lanes), low),
            vm((chips, lines, lanes), low), vm((count, lines, lanes), low),
            vm((QUARTERS, lines, wider), low), vm((others, lines, wider), low), vm((lines, wider), low),
            vm((extra, lines, wider), low), vm((QUARTERS, lines, wider), low),
            vm((lines, lanes), low), vm((extra, lines, lanes), low), vm((QUARTERS, lines, lanes), low),
            vm((chips,) + ours, low), vm((chips,) + ours, low), vm((chips,) + ours, low), vm((count,) + ours, low),
            vm(near_part.shape, low), vm((rows, width), single), vm((rows, width), single), vm((rows, width), low),
            vm((rows, width), single), vm(gate.shape, single), vm(result.shape, low),
            vm((slows,) + gwin.shape[2:], low), vm(ra.shape, low), vm((slows,) + gwin.shape[2:], low),
            vm((fasts,) + gwout.shape[2:], low), vm(rb.shape, low), vm((fasts,) + gwout.shape[2:], low),
            sem((13 + NEAR,)), sem((2,)), sem((2,)), sem((chips,)), sem((chips,)), sem((count,)), sem((count,)),
            sem((others,)), sem((others,)), sem((count,)), sem((count,)),
            sem((others,)), sem((others,)), sem((extra,)), sem((extra,)), sem((others,)), sem((others,)),
            sem((extra,)), sem((extra,)), sem((others,)), sem((others,)),
            sem((slows - 1,)), sem((slows - 1,)), sem((fasts - 1,)), sem((fasts - 1,)),
            sem((chips - NEAR, 2)), sem((chips - NEAR, 2)),
        ],
        compiler_params=pltpu.CompilerParams(collective_id=1, has_side_effects=True, vmem_limit_bytes=vmem_cap),
        cost_estimate=pl.CostEstimate(flops=0, bytes_accessed=200_000_000, transcendentals=0),
        name="reduce_all",
    )(*args)


def finish_kernel(ka_ref, la_ref, kb_ref, lb_ref, early_ref, late_ref, small_ref, gt_ref, mix_ref, *outs):
    ea_ref, eb_ref, q_ref, k_ref, v_ref, o_ref, router_ref, attn_ref, moe_ref, table_ref, gt_out, mix_out = outs
    gt_out[...] = gt_ref[...]
    mix_out[...] = mix_ref[...]
    width = q_ref.shape[2]
    experts = router_ref.shape[0]
    ea_ref[...] = ka_ref[...].astype(single) + jnp.sum(la_ref[...].astype(single), axis=0)
    eb_ref[...] = kb_ref[...].astype(single) + jnp.sum(lb_ref[...].astype(single), axis=0)
    half = width // 2
    o_ref[...] = early_ref[:, :, :width].astype(single)
    for i, ref in enumerate((q_ref, k_ref, v_ref)):
        ref[:, :, :half] = early_ref[:, :, width + i * half : width + (i + 1) * half].astype(single)
        ref[:, :, half:] = late_ref[:, :, i * half : (i + 1) * half].astype(single)

    @pl.when(pl.program_id(0) == 0)
    def _():
        small = small_ref[...].astype(single).reshape(router_ref.shape[1], TILE)
        turned = small.T
        router_ref[...] = turned[:experts]
        attn_ref[...] = turned[experts : experts + 1]
        moe_ref[...] = turned[experts + 1 : experts + 2]
        table_ref[...] = small[: table_ref.shape[0], experts + 2 : experts + 2 + table_ref.shape[1]]


def finish(ka, la, kb, lb, early, late, grad_tokens, mixed, experts, table_rows, heads):
    shape = jax.ShapeDtypeStruct
    _, lines, wider = early.shape
    lanes = late.shape[2]
    width = kb.shape[1]
    rows = QUARTERS * lines
    steps = QUARTERS
    a_cols, b_rows = ka.shape[1] // steps, kb.shape[0] // steps
    part = pl.BlockSpec((1, lines, width), lambda i: (i, 0, 0))
    once = lambda *dims: pl.BlockSpec(dims, lambda i: (0,) * len(dims))
    some = pl.BlockSpec((mixed.shape[0] // steps, width), lambda i: (i, 0))
    return pl.pallas_call(
        finish_kernel,
        grid=(steps,),
        out_shape=(
            shape(ka.shape, single), shape(kb.shape, single), *(shape((QUARTERS, lines, width), single),) * 4,
            shape((experts, rows), single), shape((1, rows), single), shape((1, rows), single),
            shape((table_rows, heads), single), shape(grad_tokens.shape, single), shape(mixed.shape, low),
        ),
        in_specs=[
            pl.BlockSpec((ka.shape[0], a_cols), lambda i: (0, i)),
            pl.BlockSpec((la.shape[0], ka.shape[0], a_cols), lambda i: (0, 0, i)),
            pl.BlockSpec((b_rows, width), lambda i: (i, 0)),
            pl.BlockSpec((lb.shape[0], b_rows, width), lambda i: (0, i, 0)),
            pl.BlockSpec((1, lines, wider), lambda i: (i, 0, 0)), pl.BlockSpec((1, lines, lanes), lambda i: (i, 0, 0)),
            pl.BlockSpec((QUARTERS, lines, TILE), lambda i: (0, 0, lanes // TILE - 1)), some, some,
        ],
        out_specs=(
            pl.BlockSpec((ka.shape[0], a_cols), lambda i: (0, i)), pl.BlockSpec((b_rows, width), lambda i: (i, 0)),
            part, part, part, part, once(experts, rows), once(1, rows), once(1, rows), once(table_rows, heads),
            some, some,
        ),
        compiler_params=pltpu.CompilerParams(vmem_limit_bytes=vmem_cap),
        cost_estimate=pl.CostEstimate(flops=0, bytes_accessed=12_000_000, transcendentals=0),
        name="finish",
    )(ka, la, kb, lb, early, late, late, grad_tokens, mixed)


def local(
    tokens,
    routes,
    slot_ids,
    w_query,
    w_key,
    w_value,
    w_output,
    w_router,
    norm_attn,
    norm_moe,
    rel_table,
    w_in,
    w_out,
    cotangent,
):
    shard_count = lax.axis_size("shard")
    token_rows, model_width = tokens.shape
    prompt_len = PR_DEV * shard_count
    weight_rows, expert_count = w_router.shape
    table_rows, head_count = rel_table.shape
    capacity = 2 * token_rows // expert_count
    slot_count = expert_count * capacity

    small = jnp.concatenate(
        [w_router, norm_attn[:, None], norm_moe[:, None],
         jnp.pad(rel_table, ((0, weight_rows - table_rows), (0, 0)))], axis=1
    )
    small = jnp.pad(small, ((0, 0), (0, TILE - small.shape[1])))
    dispatch = routes * capacity + slot_ids

    ints = jnp.concatenate([routes[None], dispatch[None], jnp.zeros((6, token_rows), jnp.int32)])
    bucket_row = jnp.asarray(np.tile(distance_buckets(table_rows * shard_count), (8, 1)), jnp.int32)
    (
        lse, rev, gate, col_slots, gains, slots_out, grad_in, weights, every_tok, small, normed, queries, keys, values,
        attended, mid,
    ) = front(ints, bucket_row, cotangent, (w_query, w_key, w_value, w_output), tokens, small, slot_count)
    by_chip = (shard_count // 2, 2, capacity, model_width)
    grad_back, result, grad_w_in, grad_w_out, router_grads = moe(
        slots_out.reshape(by_chip), grad_in.reshape(by_chip), small, w_in[0], w_out[0]
    )
    rep_count = lax.axis_size("rep")
    slows, fasts = rep_places()[3:]
    gwin = grad_w_in.reshape(slows, fasts, model_width // rep_count, -1)
    gwout = grad_w_out.reshape(slows, fasts, -1, model_width)
    early_part, dense, prompt_part, near_part, grad_own, grad_resid, ra, rb, returned = back(
        grad_back.reshape(slot_count, model_width), col_slots, mid, cotangent, gains, every_tok, weights,
        (normed, queries, keys, values, attended, lse, rev), bucket_row, router_grads, gwin, gwout, result,
    )
    chips = shard_count // 2
    lines = weight_rows // QUARTERS
    grad_tokens, mixed, early, late, ka, la, kb, lb = reduce_all(
        gains, col_slots, dense.reshape(chips, 2, QUARTERS, lines, -1),
        prompt_part.reshape(chips, 2, PR_DEV, model_width), near_part, grad_own, grad_resid, tokens, mid, gate,
        result, returned, gwin, ra, gwout, rb,
        early_part.reshape(QUARTERS, lines, -1),
    )
    in_grad, out_grad, gq, gk, gv, go, router, gain_attn, gain_moe, table, grad_tokens, mixed = finish(
        ka, la, kb, lb, early, late, grad_tokens, mixed, expert_count, table_rows, head_count
    )
    return (
        mixed,
        grad_tokens,
        *(part.reshape(weight_rows, model_width) for part in (gq, gk, gv, go)),
        router.T,
        gain_attn[0],
        gain_moe[0],
        table,
        in_grad[None],
        out_grad[None],
    )


def solution(mesh):
    return jax.shard_map(
        local,
        mesh=mesh,
        in_specs=(
            P(("rep", "shard"), None),
            P(("rep", "shard")),
            P(("rep", "shard")),
            P("shard", None),
            P("shard", None),
            P("shard", None),
            P("shard", None),
            P("shard", None),
            P("shard"),
            P("shard"),
            P("shard", None),
            P("shard", None, None),
            P("shard", None, None),
            P(("rep", "shard"), None),
        ),
        out_specs=(
            P(("rep", "shard"), None),
            P(("rep", "shard"), None),
            P("shard", None),
            P("shard", None),
            P("shard", None),
            P("shard", None),
            P("shard", None),
            P("shard"),
            P("shard"),
            P("shard", None),
            P("shard", "rep", None),
            P("shard", "rep", None),
        ),
        check_vma=False,
    )
```

profile of v0, /device:TPU:0, one launch (start us, length us, event | category | flops | bytes accessed | tf_op | source)
XLA Modules:
  0.0 252.9 jit_solution(8012141098852098459)
XLA Ops:
  0.7 0.1 pad.16.clone
  0.7 0.7 broadcast_in_dim.21
  1.4 0.7 multiply_add_fusion
  2.1 0.8 copy.30
  2.9 0.7 fusion.1
  3.6 0.7 add_add_fusion.ints_ref
  4.3 0.1 copy.31
  4.4 0.6 pad.9.little_hbm
  5.0 65.7 %front.1 = (f32[16,384]{1,0:T(8,128)}, f32[16,512]{1,0:T(8,128)}, f32[384,128]{1,0:T(8,128)}, s32[384,128]{1,0:T(8,128)}, f32[8,768]{1,0:T(8,128)}, /*index=5*/b...) custom-call(s32[8,384]{1,0:T(8,128)} %add_add_fusion.ints_ref, ...), custom_call_target="tpu_custom_call" | custom-call | flops 30000001024 | bytes 20000000 | tf_op jit(solution)/shard_map/front/pallas_call | solution.py:397
  70.7 52.6 %moe.1 = (bf16[4,2,96,768]{3,2,1,0:T(8,128)(2,1)}, bf16[4,2,96,768]{3,2,1,0:T(8,128)(2,1)}, bf16[768,3072]{1,0:T(8,128)(2,1)}, bf16[3072,768]{1,0:T(8,128)(2,1)}, f32[768,128]{1,0:T(8,128)}) custom-call(bf16[4,2,96,768]{3,2,1,0:T(8,128)(2,1)} %bitcast.42, bf16[4,2,96,768]{3,2,1,0:T(8,128)(2,1)} %bitcast.43, bf16[768,128]{1,0:T(8,128)(2,1)} %get-tuple-element.68.small_ref, ...), custom_call_target="tpu_custom_call" | custom-call | flops 40000000000 | bytes 40000000 | tf_op jit(solution)/shard_map/moe/pallas_call | solution.py:570
  123.4 64.6 %back.1 = (bf16[96,1920]{1,0:T(8,128)(2,1)}, bf16[768,1280]{1,0:T(8,128)(2,1)}, bf16[1024,768]{1,0:T(8,128)(2,1)}, bf16[256,768]{1,0:T(8,128)(2,1)}, f32[384,768...) custom-call(s32[384,128]{1,0:T(8,128)} %get-tuple-element.63.col_ref, ...), custom_call_target="tpu_custom_call" | custom-call | flops 60000002048 | bytes 40000000 | tf_op jit(solution)/shard_map/back/pallas_call | solution.py:857
  188.0 58.1 %reduce_all.1 = (f32[384,768]{1,0:T(8,128)}, bf16[384,768]{1,0:T(8,128)(2,1)}, bf16[4,24,1920]{2,1,0:T(8,128)(2,1)}, bf16[4,24,1280]{2,1,0:T(8,128)(2,1)}, bf16[...) custom-call(f32[8,768]{1,0:T(8,128)} %get-tuple-element.62.gain_ref,, ...), custom_call_target="tpu_custom_call" | custom-call | bytes 200000000 | tf_op jit(solution)/shard_map/reduce_all/pallas_call | solution.py:1125
  246.1 6.6 %finish.1 = (f32[192,3072]{1,0:T(8,128)}, f32[768,768]{1,0:T(8,128)}, f32[4,24,768]{2,1,0:T(8,128)}, f32[4,24,768]{2,1,0:T(8,128)}, f32[4,24,768]{2,1,0:T(8,128)...) custom-call(bf16[192,3072]{1,0:T(8,128)(2,1)} %get-tuple-element.92., ...), custom_call_target="tpu_custom_call" | custom-call | bytes 12000000 | tf_op jit(solution)/shard_map/finish/pallas_call | solution.py:1195
  (2 shorter events, 0.0 us)
where the time goes:
time: 253 us
  Pallas kernels  248 us (98%)
    pallas_call x1, Pallas kernels, front(): pl.pallas_call(front_kernel, out_shape=(shape((16, rows), single), shape(...  65.7 us
    pallas_call x1, Pallas kernels, back(): pl.pallas_call(back_kernel, out_shape=(shape((lines, width + 3 * early),...  64.6 us
    pallas_call x1, Pallas kernels, reduce_all(): pl.pallas_call(reduce_kernel, out_shape=(shape((rows, width), single), sh...  58.1 us
    pallas_call x1, Pallas kernels, moe(): pl.pallas_call(moe_kernel, out_shape=(shape(rows_out.shape, low), shape(r...  52.6 us
    pallas_call x1, Pallas kernels, finish(): pl.pallas_call(finish_kernel, grid=(steps,), out_shape=(shape(ka.shape, s...  6.58 us

commit v1 on v0

--- a/solution.py
+++ b/solution.py
@@ -9,7 +9,6 @@
 PR_DEV = 128
 TILE = 128
 SPAN = 2 * TILE
-BLOCK = 1536
 NEAR = 3
 QUARTERS = 4
 far_before, far_after, causal_tile, hidden_tile, tile_kinds = 3, 4, 5, 6, 7
@@ -425,16 +424,20 @@
 
 def moe_kernel(
     x_ref, g_ref, small_ref, w_in_ref, w_out_ref,
-    back_ref, out_ref, gwin_ref, gwout_ref, rg_ref,
-    w_in, w_out, xin, gm, gg, hid, gpre, logit_grads, x_t, gwin, gwout,
-    xs, xr, ms, mr, ws, ls, os_in, os_out,
+    back_ref, out_ref, ge_hbm, rx_hbm, ry_hbm, rg_ref,
+    w_in, w_out, xin, gm, gg, hid, gpre, logit_grads, x_t, gw_in, gw_out,
+    xs, xr, ms, mr, ws, ls, os_in, os_out, ex_s, ex_r, ey_s, ey_r,
 ):
     rep, chip, core, chips, quarter = places()
     experts = chips * 2
     here = chip * 2 + core
     pair_rows = 2 * xin.shape[2]
     hidden = w_in_ref.shape[1]
-    block = BLOCK
+    width = w_in_ref.shape[0]
+    _, slow, fast, slows, fasts = rep_places()
+    lines = gw_in.shape[3]
+    beside = [(slow * fasts + (fast + j) % fasts, here) for j in range(1, fasts)]
+    beyond = [((slow + j) % slows * fasts + fast, here) for j in range(1, slows)]
     loads = [
         pltpu.make_async_copy(w_in_ref, w_in, ws.at[0]),
         pltpu.make_async_copy(w_out_ref, w_out, ws.at[1]),
@@ -445,7 +448,7 @@
     targets = [
         (k, side, (rep, chip_across(chip, k) * 2 + side)) for k in range(1, chips) for side in range(2)
     ]
-    greet([twin] + [device for _, _, device in targets])
+    greet([twin] + [device for _, _, device in targets] + beside + beyond)
     sent = [send(x_ref.at[chip, 1 - core], xin.at[chip, core], (xs.at[0, 0], xr.at[0, core]), twin)]
     for k, side, device in targets:
         sent.append(
@@ -523,19 +526,39 @@
     x_t[...] = every.T
 
     def strip_writes(part):
-        cols = pl.ds(pl.multiple_of(part * block, block), block)
+        rows = pl.ds(pl.multiple_of(part * lines, lines), lines)
+        tail = pl.ds(4 * lines, 4 * lines)
+        if gw_out.shape[1] == 1:
+            second = (gw_out.at[part, 0], ge_hbm.at[part // fasts, part % fasts, tail])
+        else:
+            second = (gw_out.at[part], ge_hbm.at[part, :, tail])
         return [
-            pltpu.make_async_copy(gwin.at[:, cols], gwin_ref.at[:, cols], os_in.at[part]),
-            pltpu.make_async_copy(gwout.at[cols], gwout_ref.at[cols], os_out.at[part]),
+            pltpu.make_async_copy(gw_in.at[part], ge_hbm.at[:, :, rows], os_in.at[part]),
+            pltpu.make_async_copy(*second, os_out.at[part]),
         ]
 
-    @pl.loop(0, hidden // block)
+    grads_out = [
+        send(gw_in.at[0, :, (fast + j + 1) % fasts], rx_hbm.at[j], (ex_s.at[j], ex_r.at[j]), device)
+        for j, device in enumerate(beside)
+    ], [
+        send(gw_in.at[1, (slow + j + 1) % slows], ry_hbm.at[j], (ey_s.at[j], ey_r.at[j]), device)
+        for j, device in enumerate(beyond)
+    ]
+
+    @pl.loop(0, hidden // width)
     def strip(part):
-        cols = pl.ds(pl.multiple_of(part * block, block), block)
+        cols = pl.ds(pl.multiple_of(part * width, width), width)
         first, second = strip_writes(part)
-        gwin[:, cols] = nn(x_t[...], gpre[:, cols]).astype(low)
+        gw_in[part] = nn(x_t[...], gpre[:, cols]).astype(low).reshape(gw_in.shape[1:])
         first.start()
-        gwout[cols, :] = tn(hid[:, cols], gg[...]).astype(low)
+        for turn in range(2):
+
+            @pl.when(part == turn)
+            def _():
+                for copy in grads_out[turn]:
+                    copy.start()
+
+        gw_out[part] = tn(hid[:, cols], gg[...]).astype(low).reshape(gw_out.shape[1:])
         second.start()
 
     rg_ref[...] = sum(nn(x_t[...], part) for part in thirds_of(logit_grads[...]))
@@ -551,9 +574,11 @@
             replied(k, chip_across(chip, k), side)
     for copy in sent:
         copy.wait_send()
-    for part in range(hidden // block):
+    for part in range(hidden // width):
         for copy in strip_writes(part):
             copy.wait()
+    for copy in grads_out[0] + grads_out[1]:
+        copy.wait()
     send(gm.at[chip, 0], back_ref.at[chip, core], (ms.at[0, 0], mr.at[0, 0]), twin).wait_send()
     for k in range(1, chips):
         for side in range(2):
@@ -566,22 +591,28 @@
     hidden = w_in.shape[1]
     shape = jax.ShapeDtypeStruct
     pairs = pltpu.SemaphoreType.DMA
-    strips = hidden // BLOCK
+    strips = hidden // width
+    slows, fasts = rep_places()[3:]
+    lines = width // (slows * fasts)
     return pl.pallas_call(
         moe_kernel,
         out_shape=(
-            shape(rows_out.shape, low), shape(rows_out.shape, low), shape((width, hidden), low),
-            shape((hidden, width), low), shape((width, TILE), single),
+            shape(rows_out.shape, low), shape(rows_out.shape, low), shape((slows, fasts, 8 * lines, width), low),
+            shape((fasts - 1, slows, lines, width), low), shape((slows - 1, fasts, lines, width), low),
+            shape((width, TILE), single),
         ),
         in_specs=[in_vmem] * 3 + [anywhere] * 2,
-        out_specs=(anywhere, in_vmem, anywhere, anywhere, in_vmem),
+        out_specs=(anywhere, in_vmem, anywhere, anywhere, anywhere, in_vmem),
         scratch_shapes=[
             pltpu.VMEM((width, hidden), low), pltpu.VMEM((hidden, width), low),
             pltpu.VMEM(rows_out.shape, low), pltpu.VMEM(rows_out.shape, low), pltpu.VMEM((slots, width), low),
             pltpu.VMEM((slots, hidden), low), pltpu.VMEM((slots, hidden), low),
-            pltpu.VMEM((slots, TILE), single), pltpu.VMEM((width, slots), low), pltpu.VMEM((width, hidden), low), pltpu.VMEM((hidden, width), low),
+            pltpu.VMEM((slots, TILE), single), pltpu.VMEM((width, slots), low),
+            pltpu.VMEM((strips, slows, fasts, lines, width), low),
+            pltpu.VMEM((strips, width // (4 * lines), 4 * lines, width), low),
             pairs((chips, 2)), pairs((chips, 2)), pairs((chips, 2)), pairs((chips, 2)), pairs((2,)), pairs,
-            pairs((strips,)), pairs((strips,)),
+            pairs((strips,)), pairs((strips,)), pairs((fasts - 1,)), pairs((fasts - 1,)), pairs((slows - 1,)),
+            pairs((slows - 1,)),
         ],
         compiler_params=pltpu.CompilerParams(collective_id=3, has_side_effects=True, vmem_limit_bytes=vmem_cap),
         cost_estimate=pl.CostEstimate(flops=40_000_000_000, bytes_accessed=40_000_000, transcendentals=3_000_000),
@@ -591,13 +622,13 @@
 
 def back_kernel(
     col_ref, gain_ref, lse_ref, rev_ref, bucket_ref, rg_ref, back_hbm, mid_hbm, cot_hbm, q_hbm, k_hbm, v_hbm, o_hbm,
-    every_hbm, w_hbm, n_hbm, gwin_hbm, gwout_hbm, out_hbm,
-    z_ref, dense_hbm, p_hbm, e_hbm, own_hbm, gres_hbm, ra_hbm, rb_hbm, ret_hbm,
+    every_hbm, w_hbm, n_hbm, ge_hbm, rx_hbm, ry_hbm, out_hbm,
+    z_ref, kx_ref, ky_ref, dense_hbm, p_hbm, e_hbm, own_hbm, gres_hbm, ra_hbm, rb_hbm, ret_hbm, lx_hbm, ly_hbm,
     tiles, sums, diag, kt, dqt, far_sums, g_ref, dq_ref, dk_ref, dv_ref, attn_gain,
     every_ref, w_ref, n_ref, back_ref, mid_ref, cot_ref, q_ref, k_ref, v_ref, o_ref,
     dense_ref, own_ref, gres_ref,
-    o_grad, o_half, o_sum, o_in, h_grad, h_half, h_sum, h_in,
-    loc, out, xs, xr, as_, ar, bs, br, os_, or_, oz_s, oz_r, hs_, hr_, hz_s, hz_r,
+    x_own, x_in, x_sum, y_own, y_in, y_sum, o_grad, o_half, o_sum, o_in, h_grad, h_half, h_sum, h_in,
+    loc, out, lx_s, lx_r, ly_s, ly_r, xs, xr, as_, ar, bs, br, os_, or_, oz_s, oz_r, hs_, hr_, hz_s, hz_r,
 ):
     shard_id = lax.axis_index("shard")
     shards = lax.axis_size("shard")
@@ -609,12 +640,15 @@
     rep, slow, fast, slows, fasts = rep_places()
     _, chip, core, chips, _ = places()
     along, _, twin = peer_lists()
+    lines = x_own.shape[1]
     loads = [
         pltpu.make_async_copy(source, target, loc.at[i])
         for i, (source, target) in enumerate((
             (back_hbm, back_ref), (mid_hbm, mid_ref), (cot_hbm, cot_ref), (w_hbm.at[3], w_ref.at[3]), (o_hbm, o_ref),
             (q_hbm, q_ref), (k_hbm, k_ref), (v_hbm, v_ref), (n_hbm, n_ref), (w_hbm.at[pl.ds(0, 3)], w_ref.at[pl.ds(0, 3)]),
             (every_hbm, every_ref), (out_hbm.at[chip, core], ret_hbm.at[chip, core]),
+            (ge_hbm.at[:, fast, pl.ds(0, lines)], x_own), (rx_hbm, x_in),
+            (ge_hbm.at[slow, :, pl.ds(lines, lines)], y_own), (ry_hbm, y_in),
         ))
     ]
     for copy in loads:
@@ -631,10 +665,10 @@
     far_twins = [(rep, (chip + k) % chips * 2 + 1 - core) for k in range(1, chips)]
     greet([twin] + along + far_twins + beside + beyond)
     sent = [
-        send(gwin_hbm.at[:, (fast + j + 1) % fasts], ra_hbm.at[j], (as_.at[j], ar.at[j]), device)
+        send(ge_hbm.at[:, (fast + j + 1) % fasts, pl.ds(2 * lines, 3 * lines)], ra_hbm.at[j], (as_.at[j], ar.at[j]), device)
         for j, device in enumerate(beside)
     ] + [
-        send(gwout_hbm.at[(slow + j + 1) % slows], rb_hbm.at[j], (bs.at[j], br.at[j]), device)
+        send(ge_hbm.at[(slow + j + 1) % slows, :, pl.ds(5 * lines, 3 * lines)], rb_hbm.at[j], (bs.at[j], br.at[j]), device)
         for j, device in enumerate(beyond)
     ] + [
         send(out_hbm.at[chip_across(chip, k), side if k else 1 - core], ret_hbm.at[chip, core], (xs.at[k, side], xr.at[k, core]), device)
@@ -642,6 +676,24 @@
     ]
     for copy in sent:
         copy.start()
+    for copy in loads[12:]:
+        copy.wait()
+    for held, came, total in ((x_own, x_in, x_sum), (y_own, y_in, y_sum)):
+        value = held[...].astype(single)
+        for j in range(came.shape[0]):
+            value = value + came[j].astype(single)
+        total[...] = value.astype(low)
+    second = [
+        send(x_sum.at[(slow + j + 1) % slows], lx_hbm.at[j], (lx_s.at[j], lx_r.at[j]), device)
+        for j, device in enumerate(beyond)
+    ] + [
+        send(y_sum.at[(fast + j + 1) % fasts], ly_hbm.at[j], (ly_s.at[j], ly_r.at[j]), device)
+        for j, device in enumerate(beside)
+    ]
+    for copy in second:
+        copy.start()
+    kx_ref[...] = x_sum[slow]
+    ky_ref[...] = y_sum[fast]
     diag[...] = jnp.zeros_like(diag)
     far_sums[...] = jnp.zeros_like(far_sums)
     tile_rows = lax.broadcasted_iota(jnp.int32, (TILE, TILE), 0)
@@ -672,7 +724,7 @@
         send(h_sum.at[(chip + k + 1) % chips], h_in.at[k], (hz_s.at[k], hz_r.at[k]), device)
         for k, device in enumerate(along)
     ]
-    for copy in loads[5:]:
+    for copy in loads[5:12]:
         copy.wait()
     own = pl.ds(pl.multiple_of(shard_id * TILE, TILE), TILE)
     tail = slice((blocks + 2) * TILE, (blocks + 4) * TILE)
@@ -834,37 +886,41 @@
         send(ra_hbm.at[j], ra_hbm.at[j], (as_.at[j], ar.at[j]), twin).wait_recv()
     for j in range(slows - 1):
         send(rb_hbm.at[j], rb_hbm.at[j], (bs.at[j], br.at[j]), twin).wait_recv()
+    for copy in second:
+        copy.wait()
     for copy in sent:
         copy.wait_send()
 
 
 def back(
-    returned, col_slots, mid, cotangent, gains, every_tok, weights, kept, bucket_row, router_grads, gwin, gwout, result
+    returned, col_slots, mid, cotangent, gains, every_tok, weights, kept, bucket_row, router_grads, grads, rx, ry, result
 ):
     rows, width = mid.shape
     normed, queries, keys, values, attended, lse, rev = kept
     count = keys.shape[0]
     shards = lax.axis_size("shard")
-    slows, fasts = gwin.shape[:2]
+    slows, fasts, eighths = grads.shape[:3]
+    m = eighths // 8
     chips, lines, early = shards // 2, width // shards, width // 2
     vm = pltpu.VMEM
     shape = jax.ShapeDtypeStruct
     pairs = pltpu.SemaphoreType.DMA
     args = (
         col_slots, gains, lse, rev, bucket_row, router_grads, returned, mid, cotangent, queries, keys, values, attended,
-        every_tok, weights, normed, gwin, gwout, result,
+        every_tok, weights, normed, grads, rx, ry, result,
     )
     return pl.pallas_call(
         back_kernel,
         out_shape=(
-            shape((lines, width + 3 * early), low), shape((width, 3 * early + TILE), low),
+            shape((lines, width + 3 * early), low), shape((m, width), low), shape((m, width), low),
+            shape((width, 3 * early + TILE), low),
             shape((count - 2 * SPAN, width), low), shape((SPAN, width), low),
             shape((rows, width), single), shape((rows, width), single),
-            shape((fasts - 1, slows) + gwin.shape[2:], low), shape((slows - 1, fasts) + gwout.shape[2:], low),
-            shape(result.shape, low),
+            shape((fasts - 1, slows, 3 * m, width), low), shape((slows - 1, fasts, 3 * m, width), low),
+            shape(result.shape, low), shape((slows - 1, m, width), low), shape((fasts - 1, m, width), low),
         ),
-        in_specs=[in_vmem] * 6 + [anywhere] * 13,
-        out_specs=(in_vmem,) + (anywhere,) * 8,
+        in_specs=[in_vmem] * 6 + [anywhere] * 14,
+        out_specs=(in_vmem,) * 3 + (anywhere,) * 10,
         scratch_shapes=[
             pltpu.VMEM((2, tile_kinds, TILE, TILE), single), pltpu.VMEM((2, tile_kinds, TILE, TILE), single),
             pltpu.VMEM((16, 4 * TILE), single), pltpu.VMEM((TILE, count), low), pltpu.VMEM((TILE, rows), single),
@@ -876,11 +932,14 @@
             vm(keys.shape, low), vm(keys.shape, low), vm(attended.shape, single),
             vm((width, 3 * early + TILE), low),
             vm((rows, width), single), vm((rows, width), single),
+            vm((slows, m, width), low), vm((fasts - 1, slows, m, width), low), vm((slows, m, width), low),
+            vm((fasts, m, width), low), vm((slows - 1, fasts, m, width), low), vm((fasts, m, width), low),
             vm((shards, lines, width), low), vm((chips, lines, width), low),
             vm((chips, lines, width), low), vm((chips - 1, lines, width), low),
             vm((shards, lines, 3 * early), low), vm((chips, lines, 3 * early), low),
             vm((chips, lines, 3 * early), low), vm((chips - 1, lines, 3 * early), low),
-            pairs((12,)), pairs((6,)), pairs((NEAR, 2)), pairs((NEAR, 2)), pairs((fasts - 1,)), pairs((fasts - 1,)),
+            pairs((16,)), pairs((6,)), pairs((slows - 1,)), pairs((slows - 1,)), pairs((fasts - 1,)), pairs((fasts - 1,)),
+            pairs((NEAR, 2)), pairs((NEAR, 2)), pairs((fasts - 1,)), pairs((fasts - 1,)),
             pairs((slows - 1,)), pairs((slows - 1,)), pairs((chips,)), pairs((chips,)), pairs((chips - 1,)),
             pairs((chips - 1,)), pairs((chips,)), pairs((chips,)), pairs((chips - 1,)), pairs((chips - 1,)),
         ],
@@ -944,7 +1003,7 @@
 
 def reduce_kernel(
     gain_ref, col_ref, d_hbm, p_hbm, e_hbm, own_hbm, gres_hbm, tok_hbm, mid_hbm, gate_hbm, out_hbm, ret_hbm,
-    gwin_hbm, ra_hbm, gwout_hbm, rb_hbm, z_hbm,
+    ge_hbm, ra_hbm, rb_hbm, z_hbm,
     gt_ref, mix_ref, early_ref, late_ref, ka_ref, la_hbm, kb_ref, lb_hbm,
     d_own, half, hr, tr, mr, cr, zs, tz, z_last, z_above, z_all, last, above_in, gathered,
     p_own, p_half, p_sum, p_in, e_in, own, gres, tok, mid, gate, ret,
@@ -961,6 +1020,7 @@
     beyond = [((slow + j) % slows * fasts + fast, here) for j in range(1, slows)]
     above = [((rep // QUARTERS + k) % classes * QUARTERS + quarter, here) for k in range(1, classes)]
     wide = lambda held: held.astype(single)
+    lines = ge_hbm.shape[2] // 8
     pending = []
 
     def load(source, target, index):
@@ -977,9 +1037,9 @@
         send(piece, piece, sems, twin).wait_recv()
 
     early_in = load(z_hbm, zs, 12)
-    a_loads = [load(gwin_hbm.at[:, fast], a_own, 0), load(ra_hbm, a_in, 1)]
+    a_loads = [load(ge_hbm.at[:, fast, pl.ds(2 * lines, 3 * lines)], a_own, 0), load(ra_hbm, a_in, 1)]
     halves = [load(d_hbm.at[:, core], d_own, 5), load(p_hbm.at[:, core], p_own, 4)]
-    b_loads = [load(gwout_hbm.at[slow], b_own, 2), load(rb_hbm, b_in, 3)]
+    b_loads = [load(ge_hbm.at[slow, :, pl.ds(5 * lines, 3 * lines)], b_own, 2), load(rb_hbm, b_in, 3)]
     rest = [
         load(ret_hbm.at[chip_across(chip, k)], ret.at[chip_across(chip, k)], 13 + k) for k in range(NEAR)
     ] + [
@@ -1108,10 +1168,11 @@
         copy.wait_send()
 
 
-def reduce_all(gains, col_slots, dense, prompt_part, near_part, own, gres, tokens, mid, gate, result, returned, gwin, ra, gwout, rb, z):
+def reduce_all(gains, col_slots, dense, prompt_part, near_part, own, gres, tokens, mid, gate, result, returned, grads, ra, rb, z):
     chips = lax.axis_size("shard") // 2
     classes = lax.axis_size("rep") // QUARTERS
-    slows, fasts = gwin.shape[:2]
+    slows, fasts, eighths = grads.shape[:3]
+    part = (3 * eighths // 8, mid.shape[1])
     rows, width = mid.shape
     lines, lanes = dense.shape[3:]
     wider = z.shape[2]
@@ -1121,16 +1182,15 @@
     count, others = chips - 1, QUARTERS - 1
     ours = prompt_part.shape[2:]
     extra = max(classes - 1, 1)
-    args = (gains, col_slots, dense, prompt_part, near_part, own, gres, tokens, mid, gate, result, returned, gwin, ra, gwout, rb, z)
+    args = (gains, col_slots, dense, prompt_part, near_part, own, gres, tokens, mid, gate, result, returned, grads, ra, rb, z)
     return pl.pallas_call(
         reduce_kernel,
         out_shape=(
             shape((rows, width), single), shape((rows, width), low),
             shape((QUARTERS, lines, wider), low), shape((QUARTERS, lines, lanes), low),
-            shape(gwin.shape[2:], low), shape((slows - 1,) + gwin.shape[2:], low),
-            shape(gwout.shape[2:], low), shape((fasts - 1,) + gwout.shape[2:], low),
+            shape(part, low), shape((slows - 1,) + part, low), shape(part, low), shape((fasts - 1,) + part, low),
         ),
-        in_specs=[in_vmem] * 2 + [anywhere] * 15,
+        in_specs=[in_vmem] * 2 + [anywhere] * 14,
         out_specs=(in_vmem,) * 5 + (anywhere, in_vmem, anywhere),
         scratch_shapes=[
             vm((chips, QUARTERS, lines, lanes), low), vm((chips, QUARTERS, lines, lanes), low),
@@ -1142,8 +1202,8 @@
             vm((chips,) + ours, low), vm((chips,) + ours, low), vm((chips,) + ours, low), vm((count,) + ours, low),
             vm(near_part.shape, low), vm((rows, width), single), vm((rows, width), single), vm((rows, width), low),
             vm((rows, width), single), vm(gate.shape, single), vm(result.shape, low),
-            vm((slows,) + gwin.shape[2:], low), vm(ra.shape, low), vm((slows,) + gwin.shape[2:], low),
-            vm((fasts,) + gwout.shape[2:], low), vm(rb.shape, low), vm((fasts,) + gwout.shape[2:], low),
+            vm((slows,) + part, low), vm(ra.shape, low), vm((slows,) + part, low),
+            vm((fasts,) + part, low), vm(rb.shape, low), vm((fasts,) + part, low),
             sem((13 + NEAR,)), sem((2,)), sem((2,)), sem((chips,)), sem((chips,)), sem((count,)), sem((count,)),
             sem((others,)), sem((others,)), sem((count,)), sem((count,)),
             sem((others,)), sem((others,)), sem((extra,)), sem((extra,)), sem((others,)), sem((others,)),
@@ -1157,14 +1217,31 @@
     )(*args)
 
 
-def finish_kernel(ka_ref, la_ref, kb_ref, lb_ref, early_ref, late_ref, small_ref, gt_ref, mix_ref, *outs):
+def finish_kernel(
+    kx_ref, lx_ref, ky_ref, ly_ref, ka_ref, la_ref, kc_ref, lc_ref, kb_ref, lb_ref, early_ref, late_ref, small_ref, gt_ref, mix_ref, *outs
+):
     ea_ref, eb_ref, q_ref, k_ref, v_ref, o_ref, router_ref, attn_ref, moe_ref, table_ref, gt_out, mix_out = outs
     gt_out[...] = gt_ref[...]
     mix_out[...] = mix_ref[...]
     width = q_ref.shape[2]
     experts = router_ref.shape[0]
-    ea_ref[...] = ka_ref[...].astype(single) + jnp.sum(la_ref[...].astype(single), axis=0)
-    eb_ref[...] = kb_ref[...].astype(single) + jnp.sum(lb_ref[...].astype(single), axis=0)
+    step = pl.program_id(0)
+
+    def total(held, came):
+        value = held[...].reshape(ea_ref.shape).astype(single)
+        for j in range(came.shape[0]):
+            value = value + came[j].reshape(ea_ref.shape).astype(single)
+        return value
+
+    for target, first, last, sources in (
+        (ea_ref, 0, 0, (kx_ref, lx_ref)), (ea_ref, 1, 1, (ky_ref, ly_ref)), (ea_ref, 2, 3, (ka_ref, la_ref)),
+        (eb_ref, 0, 0, (kc_ref, lc_ref)), (eb_ref, 1, 3, (kb_ref, lb_ref)),
+    ):
+
+        @pl.when((step >= first) & (step <= last))
+        def _():
+            target[...] = total(*sources)
+
     half = width // 2
     o_ref[...] = early_ref[:, :, :width].astype(single)
     for i, ref in enumerate((q_ref, k_ref, v_ref)):
@@ -1181,14 +1258,19 @@
         table_ref[...] = small[: table_ref.shape[0], experts + 2 : experts + 2 + table_ref.shape[1]]
 
 
-def finish(ka, la, kb, lb, early, late, grad_tokens, mixed, experts, table_rows, heads):
+def finish(kx, lx, ky, ly, ka, la, kb, lb, early, late, grad_tokens, mixed, experts, table_rows, heads):
     shape = jax.ShapeDtypeStruct
     _, lines, wider = early.shape
     lanes = late.shape[2]
     width = kb.shape[1]
     rows = QUARTERS * lines
     steps = QUARTERS
-    a_cols, b_rows = ka.shape[1] // steps, kb.shape[0] // steps
+    m = kx.shape[0]
+    ka, kb = (part.reshape(3, m, width) for part in (ka, kb))
+    la, lb = (part.reshape(-1, 3, m, width) for part in (la, lb))
+    block = lambda pick: pl.BlockSpec((1, m, width), lambda i: (pick(i), 0, 0))
+    blocks = lambda array, pick: pl.BlockSpec((array.shape[0], 1, m, width), lambda i: (0, pick(i), 0, 0))
+    strip, rest = (lambda i: jnp.maximum(i - 2, 0)), (lambda i: jnp.maximum(i - 1, 0))
     part = pl.BlockSpec((1, lines, width), lambda i: (i, 0, 0))
     once = lambda *dims: pl.BlockSpec(dims, lambda i: (0,) * len(dims))
     some = pl.BlockSpec((mixed.shape[0] // steps, width), lambda i: (i, 0))
@@ -1196,27 +1278,25 @@
         finish_kernel,
         grid=(steps,),
         out_shape=(
-            shape(ka.shape, single), shape(kb.shape, single), *(shape((QUARTERS, lines, width), single),) * 4,
+            shape((m, steps * width), single), shape((steps * m, width), single), *(shape((QUARTERS, lines, width), single),) * 4,
             shape((experts, rows), single), shape((1, rows), single), shape((1, rows), single),
             shape((table_rows, heads), single), shape(grad_tokens.shape, single), shape(mixed.shape, low),
         ),
         in_specs=[
-            pl.BlockSpec((ka.shape[0], a_cols), lambda i: (0, i)),
-            pl.BlockSpec((la.shape[0], ka.shape[0], a_cols), lambda i: (0, 0, i)),
-            pl.BlockSpec((b_rows, width), lambda i: (i, 0)),
-            pl.BlockSpec((lb.shape[0], b_rows, width), lambda i: (0, i, 0)),
+            once(*kx.shape), once(*lx.shape), once(*ky.shape), once(*ly.shape),
+            block(strip), blocks(la, strip), block(lambda i: 2), blocks(la, lambda i: 2), block(rest), blocks(lb, rest),
             pl.BlockSpec((1, lines, wider), lambda i: (i, 0, 0)), pl.BlockSpec((1, lines, lanes), lambda i: (i, 0, 0)),
             pl.BlockSpec((QUARTERS, lines, TILE), lambda i: (0, 0, lanes // TILE - 1)), some, some,
         ],
         out_specs=(
-            pl.BlockSpec((ka.shape[0], a_cols), lambda i: (0, i)), pl.BlockSpec((b_rows, width), lambda i: (i, 0)),
+            pl.BlockSpec((m, width), lambda i: (0, i)), pl.BlockSpec((m, width), lambda i: (i, 0)),
             part, part, part, part, once(experts, rows), once(1, rows), once(1, rows), once(table_rows, heads),
             some, some,
         ),
         compiler_params=pltpu.CompilerParams(vmem_limit_bytes=vmem_cap),
         cost_estimate=pl.CostEstimate(flops=0, bytes_accessed=12_000_000, transcendentals=0),
         name="finish",
-    )(ka, la, kb, lb, early, late, late, grad_tokens, mixed)
+    )(kx, lx, ky, ly, ka, la, ka, la, kb, lb, early, late, late, grad_tokens, mixed)
 
 
 def local(
@@ -1257,27 +1337,23 @@
         attended, mid,
     ) = front(ints, bucket_row, cotangent, (w_query, w_key, w_value, w_output), tokens, small, slot_count)
     by_chip = (shard_count // 2, 2, capacity, model_width)
-    grad_back, result, grad_w_in, grad_w_out, router_grads = moe(
+    grad_back, result, grads, rx, ry, router_grads = moe(
         slots_out.reshape(by_chip), grad_in.reshape(by_chip), small, w_in[0], w_out[0]
     )
-    rep_count = lax.axis_size("rep")
-    slows, fasts = rep_places()[3:]
-    gwin = grad_w_in.reshape(slows, fasts, model_width // rep_count, -1)
-    gwout = grad_w_out.reshape(slows, fasts, -1, model_width)
-    early_part, dense, prompt_part, near_part, grad_own, grad_resid, ra, rb, returned = back(
+    early_part, kx, ky, dense, prompt_part, near_part, grad_own, grad_resid, ra, rb, returned, lx, ly = back(
         grad_back.reshape(slot_count, model_width), col_slots, mid, cotangent, gains, every_tok, weights,
-        (normed, queries, keys, values, attended, lse, rev), bucket_row, router_grads, gwin, gwout, result,
+        (normed, queries, keys, values, attended, lse, rev), bucket_row, router_grads, grads, rx, ry, result,
     )
     chips = shard_count // 2
     lines = weight_rows // QUARTERS
     grad_tokens, mixed, early, late, ka, la, kb, lb = reduce_all(
         gains, col_slots, dense.reshape(chips, 2, QUARTERS, lines, -1),
         prompt_part.reshape(chips, 2, PR_DEV, model_width), near_part, grad_own, grad_resid, tokens, mid, gate,
-        result, returned, gwin, ra, gwout, rb,
+        result, returned, grads, ra, rb,
         early_part.reshape(QUARTERS, lines, -1),
     )
     in_grad, out_grad, gq, gk, gv, go, router, gain_attn, gain_moe, table, grad_tokens, mixed = finish(
-        ka, la, kb, lb, early, late, grad_tokens, mixed, expert_count, table_rows, head_count
+        kx, lx, ky, ly, ka, la, kb, lb, early, late, grad_tokens, mixed, expert_count, table_rows, head_count
     )
     return (
         mixed,

time: 253 us -> 245 us (0.968)
  Pallas kernels: 248 us -> 239 us
    pallas_call x1, Pallas kernels: 64.6 us -> 53.5 us  [back(): pl.pallas_call(back_kernel, out_shape=(shape((lines, width + 3 * early),...]
    pallas_call x1, Pallas kernels: 52.6 us -> 61.3 us  [moe(): pl.pallas_call(moe_kernel, out_shape=(shape(rows_out.shape, low), shape(r...]
    pallas_call x1, Pallas kernels: 58.1 us -> 51.6 us  [reduce_all(): pl.pallas_call(reduce_kernel, out_shape=(shape((rows, width), single), sh...]
where the time goes in v1:
time: 245 us; the launch traced here: 244 us
  Pallas kernels  239 us (98%)
    pallas_call x1, Pallas kernels, front(): pl.pallas_call(front_kernel, out_shape=(shape((16, rows), single), shape(...  65.7 us
    pallas_call x1, Pallas kernels, moe(): pl.pallas_call(moe_kernel, out_shape=(shape(rows_out.shape, low), shape(r...  61.3 us
    pallas_call x1, Pallas kernels, back(): pl.pallas_call(back_kernel, out_shape=(shape((lines, width + 3 * early),...  53.5 us
    pallas_call x1, Pallas kernels, reduce_all(): pl.pallas_call(reduce_kernel, out_shape=(shape((rows, width), single), sh...  51.6 us
    pallas_call x1, Pallas kernels, finish(): pl.pallas_call(finish_kernel, grid=(steps,), out_shape=(shape((m, steps *...  6.99 us

profile of v1, /device:TPU:0, one launch (start us, length us, event | category | flops | bytes accessed | tf_op | source)
XLA Modules:
  0.0 244.3 jit_solution(13740728925022777289)
XLA Ops:
  0.7 0.1 pad.16.clone
  0.7 0.7 broadcast_in_dim.21
  1.4 0.7 multiply_add_fusion
  2.1 0.8 copy.30
  2.9 0.7 fusion.1
  3.6 0.7 add_add_fusion.ints_ref
  4.3 0.1 copy.31
  4.4 0.6 pad.9.little_hbm
  5.0 65.7 %front.1 = (f32[16,384]{1,0:T(8,128)}, f32[16,512]{1,0:T(8,128)}, f32[384,128]{1,0:T(8,128)}, s32[384,128]{1,0:T(8,128)}, f32[8,768]{1,0:T(8,128)}, /*index=5*/b...) custom-call(s32[8,384]{1,0:T(8,128)} %add_add_fusion.ints_ref, ...), custom_call_target="tpu_custom_call" | custom-call | flops 30000001024 | bytes 20000000 | tf_op jit(solution)/shard_map/front/pallas_call | solution.py:396
  70.8 61.3 %moe.1 = (bf16[4,2,96,768]{3,2,1,0:T(8,128)(2,1)}, bf16[4,2,96,768]{3,2,1,0:T(8,128)(2,1)}, bf16[2,2,1536,768]{3,2,1,0:T(8,128)(2,1)}, bf16[1,2,192,768]{3,2,1,0...) custom-call(bf16[4,2,96,768]{3,2,1,0:T(8,128)(2,1)} %bitcast.46, bf16[4,2,96,768]{3,2,1,0:T(8,128)(2,1)} %bitcast.47, ...), custom_call_target="tpu_custom_call" | custom-call | flops 40000000000 | bytes 40000000 | tf_op jit(solution)/shard_map/moe/pallas_call | solution.py:597
  132.0 53.5 %back.1 = (bf16[96,1920]{1,0:T(8,128)(2,1)}, bf16[192,768]{1,0:T(8,128)(2,1)}, bf16[192,768]{1,0:T(8,128)(2,1)}, bf16[768,1280]{1,0:T(8,128)(2,1)}, bf16[1024,76...) custom-call(s32[384,128]{1,0:T(8,128)} %get-tuple-element.67.col_ref, ...), custom_call_target="tpu_custom_call" | custom-call | flops 60000002048 | bytes 40000000 | tf_op jit(solution)/shard_map/back/pallas_call | solution.py:912
  185.6 51.6 %reduce_all.1 = (f32[384,768]{1,0:T(8,128)}, bf16[384,768]{1,0:T(8,128)(2,1)}, bf16[4,24,1920]{2,1,0:T(8,128)(2,1)}, bf16[4,24,1280]{2,1,0:T(8,128)(2,1)}, bf16[...) custom-call(f32[8,768]{1,0:T(8,128)} %get-tuple-element.68.gain_ref,, ...), custom_call_target="tpu_custom_call" | custom-call | bytes 200000000 | tf_op jit(solution)/shard_map/reduce_all/pallas_call | solution.py:1186
  237.1 7.0 %finish.1 = (f32[192,3072]{1,0:T(8,128)}, f32[768,768]{1,0:T(8,128)}, f32[4,24,768]{2,1,0:T(8,128)}, f32[4,24,768]{2,1,0:T(8,128)}, f32[4,24,768]{2,1,0:T(8,128)...) custom-call(bf16[192,768]{1,0:T(8,128)(2,1)} %get-tuple-element.88.k, ...), custom_call_target="tpu_custom_call" | custom-call | bytes 12000000 | tf_op jit(solution)/shard_map/finish/pallas_call | solution.py:1277
  (2 shorter events, 0.0 us)

commit v2 on v1

--- a/solution.py
+++ b/solution.py
@@ -142,7 +142,7 @@
 
 
 def front_kernel(
-    ints_ref, bucket_ref, cot_ref, wq_hbm, wk_hbm, wv_hbm, wo_hbm, tok_hbm, little_hbm,
+    ints_ref, bucket_ref, cot_ref, little_ref, wq_hbm, wk_hbm, wv_hbm, wo_hbm, tok_hbm,
     lse_ref, rev_ref, gate_ref, col_ref, gain_ref, x_ref, gin_hbm, w_hbm, every_hbm, small_hbm,
     n_hbm, q_hbm, k_hbm, v_hbm, o_hbm, mid_hbm,
     tiles, vt, sp, sl, gbuf, w_ref, every_ref, small_ref, tok_ref, shard_w, little,
@@ -172,9 +172,10 @@
     loads = [
         pltpu.make_async_copy(source, shard_w.at[i], loc.at[i])
         for i, source in enumerate((wq_hbm, wk_hbm, wv_hbm, wo_hbm))
-    ] + [pltpu.make_async_copy(tok_hbm, tok_ref, loc.at[4]), pltpu.make_async_copy(little_hbm, little, loc.at[5])]
+    ] + [pltpu.make_async_copy(tok_hbm, tok_ref, loc.at[4])]
     for copy in loads:
         copy.start()
+    little[...] = little_ref[...].astype(single).T[:lines].astype(low)
     greeted = [twin] + along
     for device in across + [(rep, (chip + k) % chips * 2 + 1 - core) for k in range(1, chips)]:
         greeted.append(device)
@@ -204,11 +205,12 @@
     small_ref[mine, :] = little[...]
     every_ref[pl.ds(pl.multiple_of(shard_id * PR_DEV, PR_DEV), PR_DEV), :] = tok_ref[:PR_DEV, :]
     every_ref[prompt_len + rest_rows :, :] = tok_ref[PR_DEV:, :]
-    ints = ints_ref[...].astype(single).T
+    dispatch = ints_ref[0:1, :] * (x_ref.shape[0] // experts) + ints_ref[1:2, :]
+    ints = jnp.concatenate([ints_ref[0:1, :], dispatch, jnp.zeros((6, rows), jnp.int32)], axis=0).astype(single).T
     route_col = ints[:, 0:1].astype(jnp.int32)
     col_ref[...] = jnp.broadcast_to(ints[:, 1:2].astype(jnp.int32), col_ref.shape)
     slots = lax.broadcasted_iota(jnp.int32, (x_ref.shape[0], rows), 0)
-    place = (slots == ints_ref[1:2, :]).astype(low)
+    place = (slots == dispatch).astype(low)
     gbuf[...] = nn(place, cot_ref[...]).astype(low).reshape(gbuf.shape)
     own_g = pltpu.make_async_copy(gbuf.at[shard_id], gin_hbm.at[shard_id], loc.at[6])
     own_g.start()
@@ -389,7 +391,7 @@
     shards = lax.axis_size("shard")
     chips, count = shards // 2, shards // 2 - 1
     keys = shards * PR_DEV + 2 * (rows - PR_DEV)
-    lines = small.shape[0]
+    lines = width // shards
     shape = jax.ShapeDtypeStruct
     sem = pltpu.SemaphoreType.DMA
     vm = pltpu.VMEM
@@ -403,7 +405,7 @@
             shape((width, keys), low), shape((rows, width), low), shape((keys, width), low),
             shape((keys, width), low), shape((width, rows), single), shape((rows, width), single),
         ),
-        in_specs=[in_vmem] * 3 + [anywhere] * 6,
+        in_specs=[in_vmem] * 4 + [anywhere] * 5,
         out_specs=(in_vmem,) * 6 + (anywhere,) * 10,
         scratch_shapes=[
             vm((2, tile_kinds, TILE, TILE), single), vm((TILE, keys), low), vm((keys - 2 * SPAN, 2 * rows), single),
@@ -419,14 +421,14 @@
         compiler_params=pltpu.CompilerParams(collective_id=2, has_side_effects=True, vmem_limit_bytes=vmem_cap),
         cost_estimate=pl.CostEstimate(flops=30_000_000_000, bytes_accessed=20_000_000, transcendentals=8_000_000),
         name="front",
-    )(ints, bucket_row, cotangent, *weights, tokens, small)
+    )(ints, bucket_row, cotangent, small, *weights, tokens)
 
 
 def moe_kernel(
-    x_ref, g_ref, small_ref, w_in_ref, w_out_ref,
-    back_ref, out_ref, ge_hbm, rx_hbm, ry_hbm, rg_ref,
-    w_in, w_out, xin, gm, gg, hid, gpre, logit_grads, x_t, gw_in, gw_out,
-    xs, xr, ms, mr, ws, ls, os_in, os_out, ex_s, ex_r, ey_s, ey_r,
+    small_ref, x_ref, g_hbm, w_in_ref, w_out_ref,
+    back_ref, out_hbm, ge_hbm, rx_hbm, ry_hbm, rg_ref,
+    w_in, w_out, xin, gm, gg, hid, gpre, logit_grads, x_t, gw_in, gw_out, g_ref, out_ref,
+    xs, xr, ms, mr, ws, ls, os_in, os_out, ex_s, ex_r, ey_s, ey_r, own, os_result,
 ):
     rep, chip, core, chips, quarter = places()
     experts = chips * 2
@@ -442,7 +444,11 @@
         pltpu.make_async_copy(w_in_ref, w_in, ws.at[0]),
         pltpu.make_async_copy(w_out_ref, w_out, ws.at[1]),
     ]
-    for copy in loads:
+    held = [
+        pltpu.make_async_copy(x_ref.at[chip, core], xin.at[chip, core], own.at[0]),
+        pltpu.make_async_copy(g_hbm, g_ref, own.at[1]),
+    ]
+    for copy in held + loads:
         copy.start()
     twin = (rep, chip * 2 + 1 - core)
     targets = [
@@ -456,8 +462,7 @@
         )
     for copy in sent[:5]:
         copy.start()
-    xin[chip, core] = x_ref[chip, core]
-    for copy in loads:
+    for copy in held + loads:
         copy.wait()
 
     def arrived(k, source, side):
@@ -497,6 +502,7 @@
         gpre[span, :] = grad_pre
         out = nn(active, w_out[...]).astype(low)
         out_ref[source] = out.reshape(out_ref.shape[1:])
+        pltpu.make_async_copy(out_ref.at[source], out_hbm.at[source], os_result.at[k]).start()
         grad_gate = jnp.sum(grads.astype(single) * out.astype(single), axis=1, keepdims=True)
         chosen = jnp.where(lanes == here, 1.0, 0.0)
         grad_logits = jnp.where(lanes < experts, gate * grad_gate * (chosen - probs), 0.0)
@@ -548,9 +554,8 @@
     @pl.loop(0, hidden // width)
     def strip(part):
         cols = pl.ds(pl.multiple_of(part * width, width), width)
-        first, second = strip_writes(part)
         gw_in[part] = nn(x_t[...], gpre[:, cols]).astype(low).reshape(gw_in.shape[1:])
-        first.start()
+        strip_writes(part)[0].start()
         for turn in range(2):
 
             @pl.when(part == turn)
@@ -558,8 +563,11 @@
                 for copy in grads_out[turn]:
                     copy.start()
 
+    @pl.loop(0, hidden // width)
+    def second_strip(part):
+        cols = pl.ds(pl.multiple_of(part * width, width), width)
         gw_out[part] = tn(hid[:, cols], gg[...]).astype(low).reshape(gw_out.shape[1:])
-        second.start()
+        strip_writes(part)[1].start()
 
     rg_ref[...] = sum(nn(x_t[...], part) for part in thirds_of(logit_grads[...]))
     pltpu.make_async_copy(gm.at[chip, core], back_ref.at[chip, core], ls).wait()
@@ -577,6 +585,9 @@
     for part in range(hidden // width):
         for copy in strip_writes(part):
             copy.wait()
+    for k in range(chips):
+        source = chip_across(chip, k)
+        pltpu.make_async_copy(out_ref.at[source], out_hbm.at[source], os_result.at[k]).wait()
     for copy in grads_out[0] + grads_out[1]:
         copy.wait()
     send(gm.at[chip, 0], back_ref.at[chip, core], (ms.at[0, 0], mr.at[0, 0]), twin).wait_send()
@@ -601,8 +612,8 @@
             shape((fasts - 1, slows, lines, width), low), shape((slows - 1, fasts, lines, width), low),
             shape((width, TILE), single),
         ),
-        in_specs=[in_vmem] * 3 + [anywhere] * 2,
-        out_specs=(anywhere, in_vmem, anywhere, anywhere, anywhere, in_vmem),
+        in_specs=[in_vmem] + [anywhere] * 4,
+        out_specs=(anywhere,) * 5 + (in_vmem,),
         scratch_shapes=[
             pltpu.VMEM((width, hidden), low), pltpu.VMEM((hidden, width), low),
             pltpu.VMEM(rows_out.shape, low), pltpu.VMEM(rows_out.shape, low), pltpu.VMEM((slots, width), low),
@@ -610,14 +621,15 @@
             pltpu.VMEM((slots, TILE), single), pltpu.VMEM((width, slots), low),
             pltpu.VMEM((strips, slows, fasts, lines, width), low),
             pltpu.VMEM((strips, width // (4 * lines), 4 * lines, width), low),
+            pltpu.VMEM(rows_out.shape, low), pltpu.VMEM(rows_out.shape, low),
             pairs((chips, 2)), pairs((chips, 2)), pairs((chips, 2)), pairs((chips, 2)), pairs((2,)), pairs,
             pairs((strips,)), pairs((strips,)), pairs((fasts - 1,)), pairs((fasts - 1,)), pairs((slows - 1,)),
-            pairs((slows - 1,)),
+            pairs((slows - 1,)), pairs((2,)), pairs((chips,)),
         ],
         compiler_params=pltpu.CompilerParams(collective_id=3, has_side_effects=True, vmem_limit_bytes=vmem_cap),
         cost_estimate=pl.CostEstimate(flops=40_000_000_000, bytes_accessed=40_000_000, transcendentals=3_000_000),
         name="moe",
-    )(rows_out, grad_in, small, w_in, w_out)
+    )(small, rows_out, grad_in, w_in, w_out)
 
 
 def back_kernel(
@@ -1004,10 +1016,10 @@
 def reduce_kernel(
     gain_ref, col_ref, d_hbm, p_hbm, e_hbm, own_hbm, gres_hbm, tok_hbm, mid_hbm, gate_hbm, out_hbm, ret_hbm,
     ge_hbm, ra_hbm, rb_hbm, z_hbm,
-    gt_ref, mix_ref, early_ref, late_ref, ka_ref, la_hbm, kb_ref, lb_hbm,
+    early_ref, late_ref, gt_hbm, mix_hbm, ka_hbm, la_hbm, kb_hbm, lb_hbm,
     d_own, half, hr, tr, mr, cr, zs, tz, z_last, z_above, z_all, last, above_in, gathered,
     p_own, p_half, p_sum, p_in, e_in, own, gres, tok, mid, gate, ret,
-    a_own, a_in, a_sum, b_own, b_in, b_sum,
+    a_own, a_in, a_sum, b_own, b_in, b_sum, gt_ref, mix_ref, out,
     loc, ps_s, ps_r, ds_s, ds_r, pz_s, pz_r, rr_s, rr_r, rz_s, rz_r, zr_s, zr_r, zh_s, zh_r, za_s, za_r,
     dh_s, dh_r, da_s, da_r, ea_s, ea_r, eb_s, eb_r, xs, xr,
 ):
@@ -1023,8 +1035,8 @@
     lines = ge_hbm.shape[2] // 8
     pending = []
 
-    def load(source, target, index):
-        copy = pltpu.make_async_copy(source, target, loc.at[index])
+    def load(source, target, index, sems=loc):
+        copy = pltpu.make_async_copy(source, target, sems.at[index])
         copy.start()
         return copy
 
@@ -1068,8 +1080,6 @@
         for j in range(fasts - 1):
             total = total + wide(a_in[j, t])
         a_sum[t] = total.astype(low)
-    for j, device in enumerate(beyond):
-        go(a_sum.at[(slow + j + 1) % slows], la_hbm.at[j], (ea_s.at[j], ea_r.at[j]), device)
     for copy in halves:
         copy.wait()
     for k in range(chips):
@@ -1090,9 +1100,6 @@
         for j in range(slows - 1):
             total = total + wide(b_in[j, t])
         b_sum[t] = total.astype(low)
-    for j, device in enumerate(beside):
-        go(b_sum.at[(fast + j + 1) % fasts], lb_hbm.at[j], (eb_s.at[j], eb_r.at[j]), device)
-
     def class_sum(held, came, s_sems, r_sems):
         total = wide(held[...])
         for j, device in enumerate(above):
@@ -1121,11 +1128,15 @@
 
     for copy in rest:
         copy.wait()
-    ka_ref[...] = a_sum[slow]
-    kb_ref[...] = b_sum[fast]
+    writes = [load(a_sum.at[slow], ka_hbm, 0, out), load(b_sum.at[fast], kb_hbm, 1, out)]
 
     for j in range(QUARTERS - 1):
         landed(tr.at[j], (rr_s.at[j], rr_r.at[j]))
+    for j, device in enumerate(beyond):
+        go(a_sum.at[(slow + j + 1) % slows], la_hbm.at[j], (ea_s.at[j], ea_r.at[j]), device)
+    for j, device in enumerate(beside):
+        go(b_sum.at[(fast + j + 1) % fasts], lb_hbm.at[j], (eb_s.at[j], eb_r.at[j]), device)
+
     for k in range(chips):
         total = wide(hr[quarter, k])
         for j in range(QUARTERS - 1):
@@ -1142,6 +1153,7 @@
         total = total + wide(p_in[k])
     grads = own[...] + jnp.concatenate([total, wide(e_in[...])], axis=0)
     gt_ref[...] = gres[...] + norm_pull(grads, wide(tok[...]), gain_ref[0:1, :])
+    writes.append(load(gt_ref, gt_hbm, 2, out))
 
     for k in range(chips - 1):
         landed(cr.at[k], (rz_s.at[k], rz_r.at[k]))
@@ -1156,6 +1168,7 @@
     slots = lax.broadcasted_iota(jnp.int32, (tok.shape[0], 2 * chips * ret.shape[2]), 1)
     chosen = nn((slots == col_ref[:, 0:1]).astype(low), ret[...].reshape(slots.shape[1], tok.shape[1]))
     mix_ref[...] = (mid[...] + gate[:, 0:1] * chosen).astype(low)
+    writes.append(load(mix_ref, mix_hbm, 3, out))
     handed(z_all, za_s, za_r)
     early_ref[...] = z_all[...]
     handed(gathered, da_s, da_r)
@@ -1164,6 +1177,8 @@
         landed(la_hbm.at[j], (ea_s.at[j], ea_r.at[j]))
     for j in range(fasts - 1):
         landed(lb_hbm.at[j], (eb_s.at[j], eb_r.at[j]))
+    for copy in writes:
+        copy.wait()
     for copy in pending:
         copy.wait_send()
 
@@ -1186,12 +1201,12 @@
     return pl.pallas_call(
         reduce_kernel,
         out_shape=(
+            shape((QUARTERS, lines, wider), low), shape((QUARTERS, lines, lanes), low),
             shape((rows, width), single), shape((rows, width), low),
-            shape((QUARTERS, lines, wider), low), shape((QUARTERS, lines, lanes), low),
             shape(part, low), shape((slows - 1,) + part, low), shape(part, low), shape((fasts - 1,) + part, low),
         ),
         in_specs=[in_vmem] * 2 + [anywhere] * 14,
-        out_specs=(in_vmem,) * 5 + (anywhere, in_vmem, anywhere),
+        out_specs=(in_vmem,) * 2 + (anywhere,) * 6,
         scratch_shapes=[
             vm((chips, QUARTERS, lines, lanes), low), vm((chips, QUARTERS, lines, lanes), low),
             vm((QUARTERS, chips, lines, lanes), low), vm((others, chips, lines, lanes), low),
@@ -1204,6 +1219,7 @@
             vm((rows, width), single), vm(gate.shape, single), vm(result.shape, low),
             vm((slows,) + part, low), vm(ra.shape, low), vm((slows,) + part, low),
             vm((fasts,) + part, low), vm(rb.shape, low), vm((fasts,) + part, low),
+            vm((rows, width), single), vm((rows, width), low), sem((4,)),
             sem((13 + NEAR,)), sem((2,)), sem((2,)), sem((chips,)), sem((chips,)), sem((count,)), sem((count,)),
             sem((others,)), sem((others,)), sem((count,)), sem((count,)),
             sem((others,)), sem((others,)), sem((extra,)), sem((extra,)), sem((others,)), sem((others,)),
@@ -1324,13 +1340,10 @@
     slot_count = expert_count * capacity
 
     small = jnp.concatenate(
-        [w_router, norm_attn[:, None], norm_moe[:, None],
-         jnp.pad(rel_table, ((0, weight_rows - table_rows), (0, 0)))], axis=1
+        [w_router.T, norm_attn[None], norm_moe[None], jnp.pad(rel_table.T, ((0, 0), (0, weight_rows - table_rows)))]
     )
-    small = jnp.pad(small, ((0, 0), (0, TILE - small.shape[1])))
-    dispatch = routes * capacity + slot_ids
-
-    ints = jnp.concatenate([routes[None], dispatch[None], jnp.zeros((6, token_rows), jnp.int32)])
+    small = jnp.pad(small, ((0, TILE - small.shape[0]), (0, TILE - weight_rows)))
+    ints = jnp.stack([routes, slot_ids])
     bucket_row = jnp.asarray(np.tile(distance_buckets(table_rows * shard_count), (8, 1)), jnp.int32)
     (
         lse, rev, gate, col_slots, gains, slots_out, grad_in, weights, every_tok, small, normed, queries, keys, values,
@@ -1346,7 +1359,7 @@
     )
     chips = shard_count // 2
     lines = weight_rows // QUARTERS
-    grad_tokens, mixed, early, late, ka, la, kb, lb = reduce_all(
+    early, late, grad_tokens, mixed, ka, la, kb, lb = reduce_all(
         gains, col_slots, dense.reshape(chips, 2, QUARTERS, lines, -1),
         prompt_part.reshape(chips, 2, PR_DEV, model_width), near_part, grad_own, grad_resid, tokens, mid, gate,
         result, returned, grads, ra, rb,

time: 245 us -> 238 us (0.971)
  Pallas kernels: 239 us -> 232 us
    pallas_call x1, Pallas kernels: 51.6 us -> 47.6 us  [reduce_all(): pl.pallas_call(reduce_kernel, out_shape=(shape((QUARTERS, lines, wider),...]
    pallas_call x1, Pallas kernels: 61.3 us -> 58.5 us  [moe(): pl.pallas_call(moe_kernel, out_shape=(shape(rows_out.shape, low), shape(r...]
where the time goes in v2:
time: 238 us; the launch traced here: 237 us
  Pallas kernels  232 us (97%)
  local copies, waits for them, and re-layouts  2.76 us (1%)
    pallas_call x1, Pallas kernels, front(): pl.pallas_call(front_kernel, out_shape=(shape((16, rows), single), shape(...  65.9 us
    pallas_call x1, Pallas kernels, moe(): pl.pallas_call(moe_kernel, out_shape=(shape(rows_out.shape, low), shape(r...  58.5 us
    pallas_call x1, Pallas kernels, back(): pl.pallas_call(back_kernel, out_shape=(shape((lines, width + 3 * early),...  53.5 us
    pallas_call x1, Pallas kernels, reduce_all(): pl.pallas_call(reduce_kernel, out_shape=(shape((QUARTERS, lines, wider),...  47.6 us
    pallas_call x1, Pallas kernels, finish(): pl.pallas_call(finish_kernel, grid=(steps,), out_shape=(shape((m, steps *...  6.99 us

profile of v2, /device:TPU:0, one launch (start us, length us, event | category | flops | bytes accessed | tf_op | source)
XLA Modules:
  0.0 237.4 jit_solution(17596778339333586255)
XLA Ops:
  0.6 0.7 stack.9
  1.3 0.7 stack.10
  2.0 0.6 pad_add_fusion.ints_ref
  2.6 0.8 copy.27
  3.4 0.7 fusion.1
  4.1 0.6 pad.9.little_ref
  4.7 65.9 %front.1 = (f32[16,384]{1,0:T(8,128)}, f32[16,512]{1,0:T(8,128)}, f32[384,128]{1,0:T(8,128)}, s32[384,128]{1,0:T(8,128)}, f32[8,768]{1,0:T(8,128)}, /*index=5*/b...) custom-call(s32[2,384]{1,0:T(2,128)} %pad_add_fusion.ints_ref, ...), custom_call_target="tpu_custom_call" | custom-call | flops 30000001024 | bytes 20000000 | tf_op jit(solution)/shard_map/front/pallas_call | solution.py:398
  70.6 58.5 %moe.1 = (bf16[4,2,96,768]{3,2,1,0:T(8,128)(2,1)}, bf16[4,2,96,768]{3,2,1,0:T(8,128)(2,1)}, bf16[2,2,1536,768]{3,2,1,0:T(8,128)(2,1)}, bf16[1,2,192,768]{3,2,1,0...) custom-call(bf16[768,128]{1,0:T(8,128)(2,1)} %get-tuple-element.71.small_ref, ...), custom_call_target="tpu_custom_call" | custom-call | flops 40000000000 | bytes 40000000 | tf_op jit(solution)/shard_map/moe/pallas_call | solution.py:608
  129.1 53.5 %back.1 = (bf16[96,1920]{1,0:T(8,128)(2,1)}, bf16[192,768]{1,0:T(8,128)(2,1)}, bf16[192,768]{1,0:T(8,128)(2,1)}, bf16[768,1280]{1,0:T(8,128)(2,1)}, bf16[1024,76...) custom-call(s32[384,128]{1,0:T(8,128)} %get-tuple-element.67.col_ref, ...), custom_call_target="tpu_custom_call" | custom-call | flops 60000002048 | bytes 40000000 | tf_op jit(solution)/shard_map/back/pallas_call | solution.py:924
  182.6 47.6 %reduce_all.1 = (bf16[4,24,1920]{2,1,0:T(8,128)(2,1)}, bf16[4,24,1280]{2,1,0:T(8,128)(2,1)}, f32[384,768]{1,0:T(8,128)}, bf16[384,768]{1,0:T(8,128)(2,1)}, bf16[...) custom-call(f32[8,768]{1,0:T(8,128)} %get-tuple-element.68.gain_ref,, ...), custom_call_target="tpu_custom_call" | custom-call | bytes 200000000 | tf_op jit(solution)/shard_map/reduce_all/pallas_call | solution.py:1201
  230.2 7.0 %finish.1 = (f32[192,3072]{1,0:T(8,128)}, f32[768,768]{1,0:T(8,128)}, f32[4,24,768]{2,1,0:T(8,128)}, f32[4,24,768]{2,1,0:T(8,128)}, f32[4,24,768]{2,1,0:T(8,128)...) custom-call(bf16[192,768]{1,0:T(8,128)(2,1)} %get-tuple-element.88.k, ...), custom_call_target="tpu_custom_call" | custom-call | bytes 12000000 | tf_op jit(solution)/shard_map/finish/pallas_call | solution.py:1293

commit v3 on v2

--- a/solution.py
+++ b/solution.py
@@ -142,7 +142,7 @@
 
 
 def front_kernel(
-    ints_ref, bucket_ref, cot_ref, little_ref, wq_hbm, wk_hbm, wv_hbm, wo_hbm, tok_hbm,
+    route_ref, slot_ref, bucket_ref, cot_ref, router_ref, first_ref, second_ref, table_ref, wq_hbm, wk_hbm, wv_hbm, wo_hbm, tok_hbm,
     lse_ref, rev_ref, gate_ref, col_ref, gain_ref, x_ref, gin_hbm, w_hbm, every_hbm, small_hbm,
     n_hbm, q_hbm, k_hbm, v_hbm, o_hbm, mid_hbm,
     tiles, vt, sp, sl, gbuf, w_ref, every_ref, small_ref, tok_ref, shard_w, little,
@@ -175,7 +175,16 @@
     ] + [pltpu.make_async_copy(tok_hbm, tok_ref, loc.at[4])]
     for copy in loads:
         copy.start()
-    little[...] = little_ref[...].astype(single).T[:lines].astype(low)
+    gains = [ref[...].astype(single).reshape(1, lines) for ref in (first_ref, second_ref)]
+    short = jnp.zeros((2 * TILE // 8 - 2 - experts, lines), single)
+    turned = jnp.concatenate([router_ref[...].astype(single), *gains, short], axis=0).astype(low)
+    lane = lambda count: lax.broadcasted_iota(jnp.int32, (count, TILE), 1)
+    line = lambda count: lax.broadcasted_iota(jnp.int32, (count, TILE), 0)
+    left = tn(turned, (line(turned.shape[0]) == lane(turned.shape[0])).astype(low))
+    heads = table_ref.shape[1]
+    table = nn(table_ref[...], (line(heads) + experts + 2 == lane(heads)).astype(low))
+    below = jnp.zeros((lines - table.shape[0], TILE), single)
+    little[...] = (left + jnp.concatenate([table, below], axis=0)).astype(low)
     greeted = [twin] + along
     for device in across + [(rep, (chip + k) % chips * 2 + 1 - core) for k in range(1, chips)]:
         greeted.append(device)
@@ -205,8 +214,9 @@
     small_ref[mine, :] = little[...]
     every_ref[pl.ds(pl.multiple_of(shard_id * PR_DEV, PR_DEV), PR_DEV), :] = tok_ref[:PR_DEV, :]
     every_ref[prompt_len + rest_rows :, :] = tok_ref[PR_DEV:, :]
-    dispatch = ints_ref[0:1, :] * (x_ref.shape[0] // experts) + ints_ref[1:2, :]
-    ints = jnp.concatenate([ints_ref[0:1, :], dispatch, jnp.zeros((6, rows), jnp.int32)], axis=0).astype(single).T
+    routes = route_ref[...].reshape(1, rows)
+    dispatch = routes * (x_ref.shape[0] // experts) + slot_ref[...].reshape(1, rows)
+    ints = jnp.concatenate([routes, dispatch, jnp.zeros((6, rows), jnp.int32)], axis=0).astype(single).T
     route_col = ints[:, 0:1].astype(jnp.int32)
     col_ref[...] = jnp.broadcast_to(ints[:, 1:2].astype(jnp.int32), col_ref.shape)
     slots = lax.broadcasted_iota(jnp.int32, (x_ref.shape[0], rows), 0)
@@ -285,11 +295,8 @@
         landed(w_ref.at[:, w_rows(source, 1 - core)], (wt_s.at[k], wt_r.at[k]))
     write(w_ref, w_hbm)
 
-    @pl.loop(0, every_ref.shape[0] // (2 * SPAN))
-    def project(part):
-        span = pl.ds(pl.multiple_of(part * 2 * SPAN, 2 * SPAN), 2 * SPAN)
-        k_ref[span, :] = nn(n_ref[span, :], w_ref[1]).astype(low)
-        v_ref[span, :] = nn(n_ref[span, :], w_ref[2]).astype(low)
+    k_ref[...] = nn(n_ref[...], w_ref[1]).astype(low)
+    v_ref[...] = nn(n_ref[...], w_ref[2]).astype(low)
 
     own = pl.ds(pl.multiple_of(shard_id * TILE, TILE), TILE)
     normed = jnp.concatenate([n_ref[own, :], n_ref[(blocks + 2) * TILE :, :]], axis=0)
@@ -386,7 +393,7 @@
     return powers / jnp.sum(powers, axis=1, keepdims=True)
 
 
-def front(ints, bucket_row, cotangent, weights, tokens, small, slot_count):
+def front(routes, slot_ids, bucket_row, cotangent, weights, tokens, rows_small, slot_count):
     rows, width = tokens.shape
     shards = lax.axis_size("shard")
     chips, count = shards // 2, shards // 2 - 1
@@ -405,7 +412,7 @@
             shape((width, keys), low), shape((rows, width), low), shape((keys, width), low),
             shape((keys, width), low), shape((width, rows), single), shape((rows, width), single),
         ),
-        in_specs=[in_vmem] * 4 + [anywhere] * 5,
+        in_specs=[in_vmem] * 8 + [anywhere] * 5,
         out_specs=(in_vmem,) * 6 + (anywhere,) * 10,
         scratch_shapes=[
             vm((2, tile_kinds, TILE, TILE), single), vm((TILE, keys), low), vm((keys - 2 * SPAN, 2 * rows), single),
@@ -421,7 +428,7 @@
         compiler_params=pltpu.CompilerParams(collective_id=2, has_side_effects=True, vmem_limit_bytes=vmem_cap),
         cost_estimate=pl.CostEstimate(flops=30_000_000_000, bytes_accessed=20_000_000, transcendentals=8_000_000),
         name="front",
-    )(ints, bucket_row, cotangent, small, *weights, tokens)
+    )(routes, slot_ids, bucket_row, cotangent, *rows_small, *weights, tokens)
 
 
 def moe_kernel(
@@ -462,7 +469,7 @@
         )
     for copy in sent[:5]:
         copy.start()
-    for copy in held + loads:
+    for copy in held + loads[:1]:
         copy.wait()
 
     def arrived(k, source, side):
@@ -491,6 +498,11 @@
         span = pl.ds(pl.multiple_of(source * pair_rows, pair_rows), pair_rows)
         gg[span, :] = gated
         pre = nn(rows, w_in[...])
+
+        @pl.when(k == 0)
+        def _():
+            loads[1].wait()
+
         grad_hidden = nt(gated, w_out[...])
         square = pre * pre
         wave = jnp.tanh(0.7978845608028654 * pre * (1.0 + 0.044715 * square))
@@ -1339,16 +1351,12 @@
     capacity = 2 * token_rows // expert_count
     slot_count = expert_count * capacity
 
-    small = jnp.concatenate(
-        [w_router.T, norm_attn[None], norm_moe[None], jnp.pad(rel_table.T, ((0, 0), (0, weight_rows - table_rows)))]
-    )
-    small = jnp.pad(small, ((0, TILE - small.shape[0]), (0, TILE - weight_rows)))
-    ints = jnp.stack([routes, slot_ids])
+    rows_small = (w_router.T, norm_attn, norm_moe, rel_table)
     bucket_row = jnp.asarray(np.tile(distance_buckets(table_rows * shard_count), (8, 1)), jnp.int32)
     (
         lse, rev, gate, col_slots, gains, slots_out, grad_in, weights, every_tok, small, normed, queries, keys, values,
         attended, mid,
-    ) = front(ints, bucket_row, cotangent, (w_query, w_key, w_value, w_output), tokens, small, slot_count)
+    ) = front(routes, slot_ids, bucket_row, cotangent, (w_query, w_key, w_value, w_output), tokens, rows_small, slot_count)
     by_chip = (shard_count // 2, 2, capacity, model_width)
     grad_back, result, grads, rx, ry, router_grads = moe(
         slots_out.reshape(by_chip), grad_in.reshape(by_chip), small, w_in[0], w_out[0]

time: 238 us -> 234 us (0.983)
  local copies, waits for them, and re-layouts: 2.76 us -> 0 us
where the time goes in v3:
time: 234 us
  Pallas kernels  233 us (100%)
    pallas_call x1, Pallas kernels, front(): pl.pallas_call(front_kernel, out_shape=(shape((16, rows), single), shape(...  65.7 us
    pallas_call x1, Pallas kernels, moe(): pl.pallas_call(moe_kernel, out_shape=(shape(rows_out.shape, low), shape(r...  58.8 us
    pallas_call x1, Pallas kernels, back(): pl.pallas_call(back_kernel, out_shape=(shape((lines, width + 3 * early),...  53.5 us
    pallas_call x1, Pallas kernels, reduce_all(): pl.pallas_call(reduce_kernel, out_shape=(shape((QUARTERS, lines, wider),...  47.6 us
    pallas_call x1, Pallas kernels, finish(): pl.pallas_call(finish_kernel, grid=(steps,), out_shape=(shape((m, steps *...  6.99 us

profile of v3, /device:TPU:0, one launch (start us, length us, event | category | flops | bytes accessed | tf_op | source)
XLA Modules:
  0.0 233.5 jit_solution(6720858539688546439)
XLA Ops:
  0.6 65.7 %front.1 = (f32[16,384]{1,0:T(8,128)}, f32[16,512]{1,0:T(8,128)}, f32[384,128]{1,0:T(8,128)}, s32[384,128]{1,0:T(8,128)}, f32[8,768]{1,0:T(8,128)}, /*index=5*/b...) custom-call(s32[384]{0:T(512)} %route_ref.1, ...), custom_call_target="tpu_custom_call" | custom-call | flops 30000001024 | bytes 20000000 | tf_op jit(solution)/shard_map/front/pallas_call | solution.py:405
  66.3 58.8 %moe.1 = (bf16[4,2,96,768]{3,2,1,0:T(8,128)(2,1)}, bf16[4,2,96,768]{3,2,1,0:T(8,128)(2,1)}, bf16[2,2,1536,768]{3,2,1,0:T(8,128)(2,1)}, bf16[1,2,192,768]{3,2,1,0...) custom-call(bf16[768,128]{1,0:T(8,128)(2,1)} %get-tuple-element.71.small_ref, ...), custom_call_target="tpu_custom_call" | custom-call | flops 40000000000 | bytes 40000000 | tf_op jit(solution)/shard_map/moe/pallas_call | solution.py:620
  125.2 53.5 %back.1 = (bf16[96,1920]{1,0:T(8,128)(2,1)}, bf16[192,768]{1,0:T(8,128)(2,1)}, bf16[192,768]{1,0:T(8,128)(2,1)}, bf16[768,1280]{1,0:T(8,128)(2,1)}, bf16[1024,76...) custom-call(s32[384,128]{1,0:T(8,128)} %get-tuple-element.67.col_ref, ...), custom_call_target="tpu_custom_call" | custom-call | flops 60000002048 | bytes 40000000 | tf_op jit(solution)/shard_map/back/pallas_call | solution.py:936
  178.7 47.6 %reduce_all.1 = (bf16[4,24,1920]{2,1,0:T(8,128)(2,1)}, bf16[4,24,1280]{2,1,0:T(8,128)(2,1)}, f32[384,768]{1,0:T(8,128)}, bf16[384,768]{1,0:T(8,128)(2,1)}, bf16[...) custom-call(f32[8,768]{1,0:T(8,128)} %get-tuple-element.68.gain_ref,, ...), custom_call_target="tpu_custom_call" | custom-call | bytes 200000000 | tf_op jit(solution)/shard_map/reduce_all/pallas_call | solution.py:1213
  226.3 7.0 %finish.1 = (f32[192,3072]{1,0:T(8,128)}, f32[768,768]{1,0:T(8,128)}, f32[4,24,768]{2,1,0:T(8,128)}, f32[4,24,768]{2,1,0:T(8,128)}, f32[4,24,768]{2,1,0:T(8,128)...) custom-call(bf16[192,768]{1,0:T(8,128)(2,1)} %get-tuple-element.88.k, ...), custom_call_target="tpu_custom_call" | custom-call | bytes 12000000 | tf_op jit(solution)/shard_map/finish/pallas_call | solution.py:1305

commit v4 on v3

--- a/solution.py
+++ b/solution.py
@@ -199,7 +199,7 @@
     def landed(piece, sems):
         send(piece, piece, sems, twin).wait_recv()
 
-    for copy in loads:
+    for copy in loads[:4]:
         copy.wait()
     mine = w_rows(chip, core)
     prompt, rest = tok_ref.at[pl.ds(0, PR_DEV)], tok_ref.at[pl.ds(PR_DEV, rest_rows)]
@@ -207,6 +207,7 @@
         go(shard_w.at[quarter], w_ref.at[quarter, mine], (wz_s.at[k], wz_r.at[k]), device)
         go(little, small_ref.at[mine], (sz_s.at[k], sz_r.at[k]), device)
     go(little, small_ref.at[mine], (st_s.at[0], st_r.at[0]), twin)
+    loads[4].wait()
     go(rest, every_ref.at[pl.ds(prompt_len, rest_rows)], (et_s.at[0], et_r.at[0]), twin)
     go(prompt, t_rows(chip, core), (tt_s.at[0], tt_r.at[0]), twin)
     go(shard_w, w_ref.at[:, mine], (wt_s.at[0], wt_r.at[0]), twin)

time: 234 us -> 234 us (level)
  no operation moved by 1% of the time
where the time goes in v4:
time: 234 us
  Pallas kernels  233 us (100%)
    pallas_call x1, Pallas kernels, front(): pl.pallas_call(front_kernel, out_shape=(shape((16, rows), single), shape(...  65.6 us
    pallas_call x1, Pallas kernels, moe(): pl.pallas_call(moe_kernel, out_shape=(shape(rows_out.shape, low), shape(r...  58.9 us
    pallas_call x1, Pallas kernels, back(): pl.pallas_call(back_kernel, out_shape=(shape((lines, width + 3 * early),...  53.7 us
    pallas_call x1, Pallas kernels, reduce_all(): pl.pallas_call(reduce_kernel, out_shape=(shape((QUARTERS, lines, wider),...  47.6 us
    pallas_call x1, Pallas kernels, finish(): pl.pallas_call(finish_kernel, grid=(steps,), out_shape=(shape((m, steps *...  6.99 us

profile of v4, /device:TPU:0, one launch (start us, length us, event | category | flops | bytes accessed | tf_op | source)
XLA Modules:
  0.0 233.7 jit_solution(11460600605152294956)
XLA Ops:
  0.6 65.6 %front.1 = (f32[16,384]{1,0:T(8,128)}, f32[16,512]{1,0:T(8,128)}, f32[384,128]{1,0:T(8,128)}, s32[384,128]{1,0:T(8,128)}, f32[8,768]{1,0:T(8,128)}, /*index=5*/b...) custom-call(s32[384]{0:T(512)} %route_ref.1, ...), custom_call_target="tpu_custom_call" | custom-call | flops 30000001024 | bytes 20000000 | tf_op jit(solution)/shard_map/front/pallas_call | solution.py:406
  66.3 58.9 %moe.1 = (bf16[4,2,96,768]{3,2,1,0:T(8,128)(2,1)}, bf16[4,2,96,768]{3,2,1,0:T(8,128)(2,1)}, bf16[2,2,1536,768]{3,2,1,0:T(8,128)(2,1)}, bf16[1,2,192,768]{3,2,1,0...) custom-call(bf16[768,128]{1,0:T(8,128)(2,1)} %get-tuple-element.71.small_ref, ...), custom_call_target="tpu_custom_call" | custom-call | flops 40000000000 | bytes 40000000 | tf_op jit(solution)/shard_map/moe/pallas_call | solution.py:621
  125.2 53.7 %back.1 = (bf16[96,1920]{1,0:T(8,128)(2,1)}, bf16[192,768]{1,0:T(8,128)(2,1)}, bf16[192,768]{1,0:T(8,128)(2,1)}, bf16[768,1280]{1,0:T(8,128)(2,1)}, bf16[1024,76...) custom-call(s32[384,128]{1,0:T(8,128)} %get-tuple-element.67.col_ref, ...), custom_call_target="tpu_custom_call" | custom-call | flops 60000002048 | bytes 40000000 | tf_op jit(solution)/shard_map/back/pallas_call | solution.py:937
  178.9 47.6 %reduce_all.1 = (bf16[4,24,1920]{2,1,0:T(8,128)(2,1)}, bf16[4,24,1280]{2,1,0:T(8,128)(2,1)}, f32[384,768]{1,0:T(8,128)}, bf16[384,768]{1,0:T(8,128)(2,1)}, bf16[...) custom-call(f32[8,768]{1,0:T(8,128)} %get-tuple-element.68.gain_ref,, ...), custom_call_target="tpu_custom_call" | custom-call | bytes 200000000 | tf_op jit(solution)/shard_map/reduce_all/pallas_call | solution.py:1214
  226.5 7.0 %finish.1 = (f32[192,3072]{1,0:T(8,128)}, f32[768,768]{1,0:T(8,128)}, f32[4,24,768]{2,1,0:T(8,128)}, f32[4,24,768]{2,1,0:T(8,128)}, f32[4,24,768]{2,1,0:T(8,128)...) custom-call(bf16[192,768]{1,0:T(8,128)(2,1)} %get-tuple-element.88.k, ...), custom_call_target="tpu_custom_call" | custom-call | bytes 12000000 | tf_op jit(solution)/shard_map/finish/pallas_call | solution.py:1306
